TPU v7x, 256 devices: a whole 4x4x8 slice. The times are simulated.
256 devices in a mesh: req: 32 (over z, x_hi, core), kvh: 4 (over y), exp: 2 (over x_lo).
Axes of the slice: x: 4 (x_hi: 2, x_lo: 2; x = x_hi * 2 + x_lo), y: 4, z: 8, core: 2. Of those that a mesh axis runs over, the one named last changes fastest.
Arguments:
- queries: bfloat16 [4096, 2048], P(('req', 'exp'), 'kvh'), may hold values from -170 to 170
- keys: bfloat16 [4096, 4, 64, 128], P(('req', 'exp'), 'kvh'), may hold values from -6 to 6
- values: bfloat16 [4096, 4, 64, 128], P(('req', 'exp'), 'kvh'), may hold values from -6 to 6
- lengths: int32 [4096], P('req'), may hold values from 2 to 64
- out_weight: bfloat16 [2048, 2048], P(('kvh', 'exp')), may hold values from -0.125 to 0.125
- residual: bfloat16 [4096, 2048], P('req'), may hold values from -54 to 54
- norm_gain: float32 [2048], replicated, may hold values from 0.5 to 2
- expert_ids: int32 [4096, 8], P('req'), may hold values from 0 to 63, as said below
- gate_weights: float32 [4096, 8], P('req'), may hold values from 0.2 to 1
- replica_map: int32 [128], replicated, may hold values from 0 to 63, as said below
- w_gate: bfloat16 [128, 2048, 384], P(('req', 'kvh'), None, 'exp')
- w_up: bfloat16 [128, 2048, 384], P(('req', 'kvh'), None, 'exp')
- w_down: bfloat16 [128, 384, 2048], P(('req', 'kvh'), 'exp')
Outputs:
- layer_out: bfloat16 [4096, 2048], P('req', ('kvh', 'exp'))
Inputs may be any that keep to these rules, and one draw needn't show every extreme that they name: `replica_map`: every one of the 64 experts is served by one or more slots; slots that serve one expert hold equal weights in w_gate, w_up and w_down. `expert_ids`: A token names 8 different experts and every expert is named by some token; among the 128 tokens of one req index no expert is named by more than 24 tokens, and in every req index some expert is named by exactly 24.
All inputs are finite; a program needn't handle non-finite values.
Results may differ from a plain program's by a relative error of at most 0.008.
Values may be sent and summed in bfloat16 or wider, within the bound.
A program may use at most 64 MiB of HBM per device.

v0:
```python
import jax
import jax.numpy as jnp
from jax import lax
from jax.sharding import PartitionSpec as P


def expert_runner(w_gate, w_up, w_down, complete, n_kvh, n_exp, block):

    def run(received):
        full = complete(received)
        lead_a = full.shape[0]
        lead_b = full.shape[1]
        d_model = w_gate.shape[1]
        rows = full.reshape(lead_a * lead_b, d_model)
        gate = jnp.dot(rows, w_gate[0], preferred_element_type=jnp.float32)
        up = jnp.dot(rows, w_up[0], preferred_element_type=jnp.float32)
        act = (jax.nn.silu(gate) * up).astype(jnp.bfloat16)
        down = jnp.dot(act, w_down[0], preferred_element_type=jnp.float32)
        terms = down.reshape(lead_a, lead_b, n_kvh, n_exp, block)
        summed = lax.psum_scatter(
            terms.astype(jnp.bfloat16), "exp", scatter_dimension=3, tiled=True
        )
        back = summed.reshape(lead_a, lead_b, n_kvh * block)
        return lax.all_to_all(back, "req", split_axis=0, concat_axis=0, tiled=True)

    return run


def shards(
    queries,
    keys,
    values,
    lengths,
    out_weight,
    residual,
    norm_gain,
    expert_ids,
    gate_weights,
    replica_map,
    w_gate,
    w_up,
    w_down,
):
    f32 = jnp.float32
    half_rows_count = queries.shape[0]
    n_rows = lengths.shape[0]
    head_dim = keys.shape[3]
    span = keys.shape[2]
    heads_here = queries.shape[1] // head_dim
    n_kvh = lax.axis_size("kvh")
    n_exp = lax.axis_size("exp")
    n_req = lax.axis_size("req")
    side = lax.axis_index("exp")
    own_lengths = lax.dynamic_slice_in_dim(lengths, side * half_rows_count, half_rows_count, 0)
    query = queries.reshape(half_rows_count, heads_here, head_dim)
    scores = jnp.einsum(
        "rhd,rpd->rhp", query, keys[:, 0], preferred_element_type=f32
    ) * head_dim ** (-0.5)
    position = lax.broadcasted_iota(jnp.int32, (1, 1, span), 2)
    valid = position < own_lengths[:, None, None]
    scores = jnp.where(valid, scores, -1e30)
    peak = jnp.max(scores, axis=-1)
    weights = jnp.where(valid, jnp.exp(scores - peak[..., None]), 0.0)
    total = jnp.sum(weights, axis=-1)
    probs = weights / total[..., None]
    numer = jnp.einsum(
        "rhp,rpd->rhd", probs, values[:, 0].astype(f32), precision=lax.Precision.HIGHEST
    )
    attended_part = numer.astype(jnp.bfloat16).reshape(half_rows_count, heads_here * head_dim)
    attended = lax.all_gather(attended_part, "exp", axis=0, tiled=True)
    cut = out_weight.shape[0]
    own_heads = lax.dynamic_slice_in_dim(attended, side * cut, cut, 1)
    d_model = out_weight.shape[1]
    block = d_model // (n_kvh * n_exp)
    attn_block = (
        lax.psum_scatter(
            lax.dot_general(
                out_weight, own_heads, (((0,), (1,)), ((), ())), preferred_element_type=f32
            ).astype(jnp.bfloat16),
            ("kvh", "exp"),
            scatter_dimension=0,
            tiled=True,
        )
        .astype(jnp.float32)
        .T
    )
    offset = lax.axis_index(("kvh", "exp")) * block
    mixed = lax.dynamic_slice_in_dim(residual, offset, block, 1).astype(f32) + attn_block
    squares = lax.psum(jnp.sum(mixed * mixed, axis=1), ("kvh", "exp"))
    scale = lax.rsqrt(squares / d_model + 1e-06)
    gain_block = lax.dynamic_slice_in_dim(norm_gain, offset, block, 0)
    normed = (mixed * scale[:, None] * gain_block[None, :]).astype(jnp.bfloat16)
    top = expert_ids.shape[1]
    n_slots = replica_map.shape[0]
    n_experts = n_slots // 2
    capacity = min(n_rows, max(2, (3 * n_rows * top + 2 * n_experts - 1) // (2 * n_experts)))
    probs_top = gate_weights / jnp.sum(gate_weights, axis=1, keepdims=True)
    expert_range = jnp.arange(n_experts, dtype=jnp.int32)
    owned = (replica_map[:, None] == expert_range[None, :]).astype(jnp.int32)
    earlier = jnp.cumsum(owned, axis=0) - owned
    rank = jnp.sum(earlier * owned, axis=1)
    copies = jnp.sum(owned, axis=0)
    picked = (expert_ids[..., None] == expert_range).astype(jnp.int32)
    copies_pair = jnp.sum(picked * copies, axis=-1)
    turn = jnp.full((n_rows, top), lax.axis_index("req"), jnp.int32)
    which = turn % copies_pair
    match = (replica_map == expert_ids[..., None]) & (rank == which[..., None])
    slot = jnp.argmax(match, axis=-1)
    mine = slot % n_kvh == lax.axis_index("kvh")
    flat_dest = (slot // n_kvh).reshape(-1)
    flat_mine = mine.reshape(-1)
    toward = (
        (flat_dest[:, None] == jnp.arange(n_req, dtype=jnp.int32)[None, :]) & flat_mine[:, None]
    ).astype(jnp.int32)
    before = jnp.cumsum(toward, axis=0) - toward
    place = jnp.sum(before * toward, axis=1)
    n_buffer = n_req * capacity
    target = jnp.where(flat_mine, flat_dest * capacity + place, n_buffer)
    row_of = jnp.arange(n_rows * top, dtype=jnp.int32) // top
    source = jnp.full((n_buffer,), -1, jnp.int32).at[target].set(row_of, mode="drop")
    full_rows = lax.all_gather(normed, ("kvh", "exp"), axis=1, tiled=True)

    def keep(received):
        return received

    runner = expert_runner(w_gate, w_up, w_down, keep, n_kvh, n_exp, block)
    taken = full_rows[jnp.maximum(source, 0)]
    returned = runner(
        lax.all_to_all(
            jnp.where(source[:, None] >= 0, taken, jnp.zeros((), jnp.bfloat16)).reshape(
                n_req, capacity, full_rows.shape[1]
            ),
            "req",
            split_axis=0,
            concat_axis=0,
            tiled=True,
        )
    )
    flat_back = returned.reshape(n_buffer, n_kvh * block)
    gathered = flat_back[jnp.minimum(target, n_buffer - 1)].reshape(n_rows, top, n_kvh * block)
    weight = jnp.where(mine, probs_top, 0.0)
    partial_value = jnp.zeros((n_rows, n_kvh * block), f32)
    for entry in range(top):
        partial_value = partial_value + weight[:, entry, None] * gathered[:, entry].astype(f32)
    moe_block = (
        lax.psum_scatter(
            partial_value.reshape(n_rows, n_kvh, block).astype(jnp.bfloat16),
            "kvh",
            scatter_dimension=1,
            tiled=True,
        )
        .astype(jnp.float32)
        .reshape(n_rows, block)
    )
    return (mixed + moe_block).astype(jnp.bfloat16)


def solution(mesh):
    in_specs = (
        P(("req", "exp"), "kvh"),
        P(("req", "exp"), "kvh", None, None),
        P(("req", "exp"), "kvh", None, None),
        P("req"),
        P(("kvh", "exp"), None),
        P("req", None),
        P(),
        P("req", None),
        P("req", None),
        P(),
        P(("req", "kvh"), None, "exp"),
        P(("req", "kvh"), None, "exp"),
        P(("req", "kvh"), "exp", None),
    )
    out_specs = P("req", ("kvh", "exp"))
    return jax.shard_map(shards, mesh=mesh, in_specs=in_specs, out_specs=out_specs, check_vma=False)
```

profile of v0, /device:TPU:6, one launch (start us, length us, event | category | flops | bytes accessed | tf_op | source)
XLA Modules:
  0.0 418.6 jit_solution(3520700671279704682)
XLA Ops:
  10.4 2.2 convolution_convert_fusion.2
  12.6 4.9 %all_gather.6 = bf16[128,512]{1,0:T(8,128)(2,1)S(1)} all-gather(bf16[64,512]{1,0:T(8,128)(2,1)S(1)} %bitcast.127), channel_id=1, replica_groups=mesh['req'=32,'kvh'=4,'exp'=2] {'exp'}, dimensions={0}, use_global_device_ids=true | all-gather | bytes 196608 | tf_op jit(solution)/shard_map/all_gather | solution.py:70
  19.6 5.6 %iota_reduce_fusion = (pred[128,8]{1,0:T(8,128)(4,1)}, s32[128,8]{1,0:T(8,128)S(1)}) fusion(s32[128,8]{1,0:T(8,128)S(1)} %copy.92, s32[128]{0:T(128)S(1)} %get-tuple-element.7, s32[128,8]{1,0:T(8,128)S(1)} %copy.91, s32[128]{0:T(128)S(1)} %copy-done.5), kind=kLoop, calls=%fused_computation.24 | loop fusion | flops 1303552 | bytes 14336 | tf_op jit(solution)/shard_map/shards/reduce | solution.py:108
  25.8 9.0 %reduce-window.6 = s32[32,8,128]{2,1,0:T(8,128)S(1)} reduce-window(s32[32,8,128]{2,1,0:T(8,128)S(1)} %fusion.21, s32[]{:T(128)} %constant.89.clone.1), window={size=1x1x128 pad=0_0x0_0x127_0}, to_apply=%region_9.10 | reduce-window | flops 4161536 | bytes 262148 | tf_op jit(solution)/shard_map/reduce-window
  35.8 4.3 %scatter_custom_fusion = s32[768]{0:T(1024)S(1)} fusion(s32[1024]{0:T(1024)S(1)} %bitcast.132, s32[1024]{0:T(1024)S(1)} %add_select_fusion, s32[]{:T(128)} %constant.107.clone.1), kind=kCustom, calls=%fused_computation.82 | custom fusion | bytes 3076 | tf_op jit(solution)/shard_map/scatter | solution.py:120
  41.0 18.8 %reduce-scatter.4.cloned.1.call-done = bf16[256,128]{0,1:T(8,128)(2,1)} async-done(((bf16[2048,128]{0,1:T(8,128)(2,1)}), bf16[256,128]{0,1:T(8,128)(2,1)}) %reduce-scatter.4.cloned.1.call-update) | async-done | bytes 65552 | tf_op jit(solution)/shard_map/reduce_scatter | solution.py:76
  60.9 19.3 %psum.7 = f32[128]{0:T(128)S(1)} all-reduce(f32[128]{0:T(128)S(1)} %multiply_reduce_fusion), channel_id=1, replica_groups=mesh['req'=32,'kvh'=4,'exp'=2] {'kvh','exp'}, use_global_device_ids=true, to_apply=%region_14.15 | all-reduce | flops 128 | bytes 1024 | tf_op jit(solution)/shard_map/psum | solution.py:89
  81.1 28.0 %all_gather.7 = bf16[128,2048]{1,0:T(8,128)(2,1)S(1)} all-gather(bf16[128,256]{1,0:T(8,128)(2,1)S(1)} %multiply_convert_fusion), channel_id=1, replica_groups=mesh['req'=32,'kvh'=4,'exp'=2] {'kvh','exp'}, dimensions={1}, use_global_device_ids=true | all-gather | bytes 589824 | tf_op jit(solution)/shard_map/all_gather | solution.py:121
  109.2 4.3 %gather_fusion = bf16[768,2048]{1,0:T(8,128)(2,1)} fusion(bf16[128,2048]{1,0:T(8,128)(2,1)S(1)} %all_gather.7, s32[1024]{0:T(1024)S(1)} %pad_clamp_fusion), kind=kCustom, calls=%fused_computation | custom fusion | bytes 6294528 | tf_op jit(solution)/shard_map/gather | solution.py:127
  113.4 3.8 broadcast_select_fusion
  117.3 10.2 %all-to-all-start = ((bf16[32,24,2048]{2,1,0:T(8,128)(2,1)}), bf16[32,24,2048]{2,1,0:T(8,128)(2,1)}, u32[]{:S(2)}, u32[]{:S(2)}) async-start(bf16[32,24,2048]{2,1,0:T(8,128)(2,1)} %broadcast_select_fusion), calls=%async_computation.1 | async-start | bytes 6291456 | tf_op jit(solution)/shard_map/all_to_all | solution.py:129
  128.3 71.3 %all-to-all-done = bf16[32,24,2048]{2,1,0:T(8,128)(2,1)} async-done(((bf16[32,24,2048]{2,1,0:T(8,128)(2,1)}), bf16[32,24,2048]{2,1,0:T(8,128)(2,1)}, u32[]{:S(2)}, u32[]{:S(2)}) %all-to-all-start) | async-done | bytes 3145760 | tf_op jit(solution)/shard_map/all_to_all | solution.py:129
  199.6 3.1 fusion.11
  202.7 3.1 fusion.2
  206.0 2.7 convolution_convert_fusion.1
  209.4 93.9 %all-reduce.3.cloned.1.call-done = bf16[32,24,4,2,256]{4,1,3,2,0:T(8,128)(2,1)} async-done(((bf16[32,24,4,2,256]{4,1,3,2,0:T(8,128)(2,1)}), bf16[32,24,4,2,256]{4,1,3,2,0:T(8,128)(2,1)}) %all-reduce.3.cloned.1.call-update) | async-done | bytes 3145744
  303.3 2.2 constant_dynamic-slice_fusion
  306.3 2.4 reshape.238
  308.6 10.1 %all-to-all-start.1 = ((bf16[32,24,1024]{2,1,0:T(8,128)(2,1)}), bf16[32,24,1024]{2,1,0:T(8,128)(2,1)S(1)}, u32[]{:S(2)}, u32[]{:S(2)}) async-start(bf16[32,24,1024]{2,1,0:T(8,128)(2,1)} %reshape.238), calls=%async_computation.2 | async-start | bytes 3145728 | tf_op jit(solution)/shard_map/all_to_all | solution.py:24
  318.8 39.1 %all-to-all-done.1 = bf16[32,24,1024]{2,1,0:T(8,128)(2,1)S(1)} async-done(((bf16[32,24,1024]{2,1,0:T(8,128)(2,1)}), bf16[32,24,1024]{2,1,0:T(8,128)(2,1)S(1)}, u32[]{:S(2)}, u32[]{:S(2)}) %all-to-all-start.1) | async-done | bytes 1572896 | tf_op jit(solution)/shard_map/all_to_all | solution.py:24
  358.0 5.4 %gather_fusion.1 = bf16[1024,1024]{1,0:T(8,128)(2,1)} fusion(bf16[768,1024]{1,0:T(8,128)(2,1)S(1)} %bitcast.113, s32[1024]{0:T(1024)S(1)} %broadcast_clamp_fusion), kind=kCustom, calls=%fused_computation.1 | custom fusion | bytes 4198400 | tf_op jit(solution)/shard_map/gather | solution.py:140
  363.3 12.5 %fusion.38 = (bf16[128,1,1024]{2,1,0:T(2,128)(2,1)S(1)}, bf16[128,1,1024]{2,1,0:T(2,128)(2,1)}, bf16[128,1,1024]{2,1,0:T(2,128)(2,1)}, bf16[128,1,1024]{2,1,0:T(...) fusion(bf16[128,8,1024]{2,1,0:T(8,128)(2,1)} %bitcast.114), kind=kLoop, calls=%fused_computation.95 | loop fusion | bytes 4194304 | tf_op jit(solution)/shard_map/slice | solution.py:144
  387.2 2.6 add_convert_fusion
  389.8 20.8 %reduce-scatter.6.cloned.1.call-done = bf16[128,1,256]{2,0,1:T(8,128)(2,1)} async-done(((bf16[128,4,256]{2,0,1:T(8,128)(2,1)}), bf16[128,1,256]{2,0,1:T(8,128)(2,1)}) %reduce-scatter.6.cloned.1.call-update) | async-done | bytes 65552 | tf_op jit(solution)/shard_map/reduce_scatter | solution.py:146
  (91 shorter events, 25.5 us)
Async XLA Ops:
  6.5 11.0 %copy-start = (bf16[256,2048]{1,0:T(8,128)(2,1)S(1)}, bf16[256,2048]{1,0:T(8,128)(2,1)}, u32[]{:S(2)}) copy-start(bf16[256,2048]{1,0:T(8,128)(2,1)} %param.17) | copy-start | bytes 3145732
  6.5 12.2 %copy-start.5 = (s32[128]{0:T(128)S(1)}, s32[128]{0:T(128)}, u32[]{:S(2)}) copy-start(s32[128]{0:T(128)} %param.22) | copy-start | bytes 1540
  6.5 12.6 %copy-start.4 = (s32[128,8]{0,1:T(8,128)S(1)}, s32[128,8]{0,1:T(8,128)}, u32[]{:S(2)}) copy-start(s32[128,8]{0,1:T(8,128)} %param.20) | copy-start | bytes 12292
  6.5 18.7 %copy-start.3 = (f32[128,8]{0,1:T(8,128)S(1)}, f32[128,8]{0,1:T(8,128)}, u32[]{:S(2)}) copy-start(f32[128,8]{0,1:T(8,128)} %param.21) | copy-start | bytes 12292
  6.5 53.3 %reduce-scatter.4.cloned.1.call-start = ((), (), s32[]{:S(2)}) async-start(), calls=%async_computation.4 | async-start | bytes 589824 | tf_op jit(solution)/shard_map/reduce_scatter | solution.py:76
  117.3 10.4 %copy-start.1 = (bf16[1,192,2048]{2,1,0:T(8,128)(2,1)S(1)}, bf16[1,192,2048]{2,1,0:T(8,128)(2,1)}, u32[]{:S(2)}) copy-start(bf16[1,192,2048]{2,1,0:T(8,128)(2,1)} %param.25) | copy-start | bytes 2359300
  117.3 82.3 %copy-start.6 = (bf16[1,2048,192]{1,2,0:T(8,128)(2,1)S(1)}, bf16[1,2048,192]{1,2,0:T(8,128)(2,1)}, u32[]{:S(2)}) copy-start(bf16[1,2048,192]{1,2,0:T(8,128)(2,1)} %param.23) | copy-start | bytes 2359300
  117.3 82.3 %all-to-all-start = ((bf16[32,24,2048]{2,1,0:T(8,128)(2,1)}), bf16[32,24,2048]{2,1,0:T(8,128)(2,1)}, u32[]{:S(2)}, u32[]{:S(2)}) async-start(bf16[32,24,2048]{2,1,0:T(8,128)(2,1)} %broadcast_select_fusion), calls=%async_computation.1 | async-start | bytes 6291456 | tf_op jit(solution)/shard_map/all_to_all | solution.py:129
  127.5 175.9 %all-reduce.3.cloned.1.call-start = ((), (), s32[]{:S(2)}) async-start(), calls=%async_computation.6 | async-start | bytes 6291456
  199.6 3.2 copy-start.7
  206.0 2.8 copy-start.8
  308.6 49.3 %all-to-all-start.1 = ((bf16[32,24,1024]{2,1,0:T(8,128)(2,1)}), bf16[32,24,1024]{2,1,0:T(8,128)(2,1)S(1)}, u32[]{:S(2)}, u32[]{:S(2)}) async-start(bf16[32,24,1024]{2,1,0:T(8,128)(2,1)} %reshape.238), calls=%async_computation.2 | async-start | bytes 3145728 | tf_op jit(solution)/shard_map/all_to_all | solution.py:24
  318.8 91.8 %reduce-scatter.6.cloned.1.call-start = ((), (), s32[]{:S(2)}) async-start(), calls=%async_computation.5 | async-start | bytes 327680 | tf_op jit(solution)/shard_map/reduce_scatter | solution.py:146
  386.6 24.0 %copy-start.2 = (bf16[256,128]{0,1:T(8,128)(2,1)S(1)}, bf16[256,128]{0,1:T(8,128)(2,1)}, u32[]{:S(2)}) copy-start(bf16[256,128]{0,1:T(8,128)(2,1)} %reduce-scatter.4.cloned.1.call-done) | copy-start | bytes 196612
Sparse Core Ops, SparseCore 0:
  18.8 41.0 reduce-scatter.3
  208.9 94.3 all-reduce.2
  389.9 20.5 reduce-scatter.5
where the time goes:
time: 419 us
  waiting for transfers between devices  244 us (58%)
  blocking collectives  52.3 us (12%)
  local copies, waits for them, and re-layouts  48.4 us (12%)
  other arithmetic  25.5 us (6%)
  starting transfers between devices  20.6 us (5%)
  matrix products  14.3 us (3%)
  between operations  13.5 us (3%)
    unnamed x4, waiting for transfers between devices  94 us
    all_to_all x1, waiting for transfers between devices, shards(): lax.all_to_all(jnp.where(source[:, None] >= 0, taken, jnp.zeros((), jnp.b...  71.3 us
    all_to_all x1, waiting for transfers between devices, run(): return lax.all_to_all(back, 'req', split_axis=0, concat_axis=0, tiled=True)  39.1 us
    all_gather x1, blocking collectives, shards(): full_rows = lax.all_gather(normed, ('kvh', 'exp'), axis=1, tiled=True)  28 us
    reduce_scatter x1, waiting for transfers between devices, shards(): lax.psum_scatter(partial_value.reshape(n_rows, n_kvh, block).astype(jnp.b...  20.8 us
    psum x1, blocking collectives, shards(): squares = lax.psum(jnp.sum(mixed * mixed, axis=1), ('kvh', 'exp'))  19.3 us
    reduce_scatter x1, waiting for transfers between devices, shards(): lax.psum_scatter(lax.dot_general(out_weight, own_heads, (((0,), (1,)), ((...  18.8 us
    slice x1, local copies, waits for them, and re-layouts, shards(): gathered[:, entry].astype(f32)  12.5 us
  transfers between devices with their start and end apart: 5, of which 5 were waited for; matrix products, arithmetic and copies ran while one was open for 6% of the time, Pallas kernels for 0%

commit v1 on v0

v1 whole, which is shorter than its diff:
```python
import jax
import jax.numpy as jnp
from jax import lax
from jax.experimental import pallas as pl
from jax.experimental.pallas import tpu as pltpu
from jax.sharding import PartitionSpec as P

MESH = pl.DeviceIdType.MESH
F32 = jnp.float32
BF16 = jnp.bfloat16

NZ = 8
CAP = 24
ORDER = (0, 1, 4, 5, 3, 6, 2, 7)
PAIRS = NZ // 2


def layer_kernel(
    q_ref,
    len_ref,
    gain_ref,
    route_ref,
    map_ref,
    k_hbm,
    v_hbm,
    ow_hbm,
    res_hbm,
    wg_hbm,
    wu_hbm,
    wd_hbm,
    out_ref,
    kbuf,
    vbuf,
    owb,
    resb,
    lens_t,
    eprim,
    att,
    oh,
    rs_send,
    rs_recv,
    mixed,
    sq_send,
    sq_recv,
    sc,
    rt,
    xg,
    dmat,
    wmat,
    send1,
    recv1,
    send2,
    recv2,
    own_sum,
    zs_send,
    zs_recv,
    wg,
    wu,
    wd,
    load_sem,
    w_send,
    w_in,
    fwd_send,
    w_other,
    att_sems,
    rs_sems,
    sq_sems,
    sc_send,
    sc_recv,
    rt_send,
    rt_recv,
    xg_send,
    xg_recv,
    a2a_send,
    a2a_recv,
    back_send,
    back_recv,
    zs_sems,
):
    req = lax.axis_index("req")
    y = lax.axis_index("kvh")
    xl = lax.axis_index("exp")
    z = lax.div(req, 4)
    xh = lax.rem(lax.div(req, 2), 2)
    c = lax.rem(req, 2)
    blk = y * 2 + xl
    slot = xh * 8 + xl * 4 + y
    swap = lax.rem(c + xl, 2)

    def plane_peer(d):
        xh_to = lax.rem(xh + lax.div(d, 8), 2)
        xl_to = lax.rem(xl + lax.rem(lax.div(d, 4), 2), 2)
        y_to = lax.rem(y + lax.rem(d, 4), 4)
        return xh_to, xl_to, y_to, (z * 4 + xh_to * 2 + c, y_to, xl_to)

    def z_peer(d):
        return (lax.rem(z + d, NZ) * 4 + xh * 2 + c, y, xl)

    other_core = (z * 4 + xh * 2 + (1 - c), y, xl)
    swap_peer = (z * 4 + xh * 2 + (1 - c), y, 1 - xl)

    barrier = pltpu.get_barrier_semaphore()

    def greet_plane(d, carry):
        pl.semaphore_signal(barrier, inc=1, device_id=plane_peer(d)[3], device_id_type=MESH)
        return carry

    lax.fori_loop(1, 16, greet_plane, 0)

    def greet_z(d, carry):
        pl.semaphore_signal(barrier, inc=1, device_id=z_peer(d), device_id_type=MESH)
        return carry

    lax.fori_loop(1, NZ, greet_z, 0)
    pl.semaphore_signal(barrier, inc=1, device_id=other_core, device_id_type=MESH)

    @pl.when(swap == 1)
    def _():
        pl.semaphore_signal(barrier, inc=1, device_id=swap_peer, device_id_type=MESH)

    def load(src, dst, i):
        return pltpu.make_async_copy(src, dst, load_sem.at[i])

    loads = [load(k_hbm, kbuf, 0), load(v_hbm, vbuf, 1)]
    loads.append(
        load(res_hbm.at[:, pl.ds(pl.multiple_of(blk * 256, 256), 256)], resb, 2)
    )
    for b in range(8):
        loads.append(load(ow_hbm.at[:, pl.ds(b * 256, 256)], owb.at[b], 3 + b))
    for one in loads:
        one.start()
    pl.semaphore_wait(barrier, 23 + swap)

    weights = ((wg_hbm, wg), (wu_hbm, wu), (wd_hbm, wd))

    def remote(src, dst, send_sem, recv_sem, device):
        return pltpu.make_async_remote_copy(
            src_ref=src,
            dst_ref=dst,
            send_sem=send_sem,
            recv_sem=recv_sem,
            device_id=device,
            device_id_type=MESH,
        )

    rt[0] = route_ref[...]
    for pos in range(1, NZ):
        remote(
            rt.at[0], rt.at[pos], rt_send.at[pos], rt_recv.at[pos], z_peer(NZ - ORDER[pos])
        ).start()

    @pl.when(swap == 0)
    def _():
        for i, (src, dst) in enumerate(weights):
            pltpu.make_async_copy(src, dst.at[c], w_in.at[i]).start()
            remote(src, dst.at[c], w_send.at[i], w_other.at[i], other_core).start()

    @pl.when(swap == 1)
    def _():
        for i, (src, dst) in enumerate(weights):
            remote(src, dst.at[1 - c], w_send.at[i], w_in.at[i], swap_peer).start()

    lens_t[...] = jnp.broadcast_to(len_ref[...].astype(F32), (128, 128)).T
    loads[0].wait()
    loads[1].wait()
    scale = 128 ** (-0.5)
    rows_at = lax.broadcasted_iota(jnp.int32, (64, 1024), 0)
    cols_at = lax.broadcasted_iota(jnp.int32, (64, 1024), 1)
    same = (rows_at & 15) == (cols_at >> 6)
    at = (cols_at & 63).astype(F32)
    for g in range(4):
        lo = g * 16
        heads = [q_ref[lo : lo + 16, h * 128 : (h + 1) * 128] for h in range(4)]
        q16 = jnp.concatenate(heads, axis=0)
        k16 = kbuf[g * 1024 : (g + 1) * 1024, :]
        s = lax.dot_general(q16, k16, (((1,), (1,)), ((), ())), preferred_element_type=F32)
        own_len = lens_t[pl.ds(pl.multiple_of(xl * 64 + lo, 16), 16), :][:, 0:1]
        live = same & (at < jnp.concatenate([own_len] * 4, axis=0))
        s = jnp.where(live, s * scale, -1e30)
        peak = jnp.max(s, axis=1, keepdims=True)
        w = jnp.where(live, jnp.exp(s - peak), 0.0)
        total = jnp.sum(w, axis=1, keepdims=True)
        v16 = vbuf[g * 1024 : (g + 1) * 1024, :]
        a = jnp.dot(w.astype(BF16), v16, preferred_element_type=F32) / total
        a = a.astype(BF16)
        for h in range(4):
            att[h // 2, lo : lo + 16, (h % 2) * 128 : (h % 2 + 1) * 128] = a[
                h * 16 : (h + 1) * 16, :
            ]
    att_copy = remote(
        att.at[1 - xl], oh.at[xl], att_sems.at[0], att_sems.at[1], (req, y, 1 - xl)
    )
    att_copy.start()
    oh[xl] = att[xl]

    row = jnp.broadcast_to(map_ref[...].astype(F32), (128, 128))
    col = row.T
    sub = lax.broadcasted_iota(jnp.int32, (128, 128), 0)
    lane = lax.broadcasted_iota(jnp.int32, (128, 128), 1)
    again = jnp.where((row == col) & (lane < sub), 1.0, 0.0)
    eprim[...] = jnp.where(jnp.max(again, axis=1, keepdims=True) > 0.0, -1.0, col)

    for i in range(2, 11):
        loads[i].wait()
    att_copy.wait()
    heads_all = oh[...].reshape(128, 256)

    def scatter(d, carry):
        to = lax.rem(blk + d, 8)
        part = jnp.dot(heads_all, owb[to], preferred_element_type=F32)
        rs_send[d - 1] = part.astype(BF16)
        remote(
            rs_send.at[d - 1],
            rs_recv.at[d - 1],
            rs_sems.at[0],
            rs_sems.at[1],
            (req, lax.div(to, 2), lax.rem(to, 2)),
        ).start()
        return carry

    lax.fori_loop(1, 8, scatter, 0)
    own_part = jnp.dot(heads_all, owb[blk], preferred_element_type=F32)

    for pos in range(1, NZ):
        remote(rt.at[0], rt.at[pos], rt_send.at[pos], rt_recv.at[pos], z_peer(NZ - ORDER[pos])).wait()
    expert = eprim[pl.ds(pl.multiple_of(z * 16, 16), 16), :]
    upper = jnp.where(sub < lane, 1.0, 0.0).astype(BF16)
    kk = lax.broadcasted_iota(jnp.int32, (2 * CAP, 256), 0).astype(F32)

    def routing(p, carry):
        places, probs = [], []
        for r in range(2):
            info = rt[2 * p + r]
            ids = info[0:8, :]
            gates = info[8:16, :]
            top = gates / jnp.sum(gates, axis=0, keepdims=True)
            named = jnp.zeros((16, 128), F32)
            prob = jnp.zeros((16, 128), F32)
            for j in range(8):
                hit = ids[j : j + 1, :] == expert
                named = jnp.where(hit, 1.0, named)
                prob = jnp.where(hit, top[j : j + 1, :], prob)
            before = jnp.dot(named.astype(BF16), upper, preferred_element_type=F32)
            places.append(jnp.where(named > 0.0, before + r * CAP, -100.0))
            probs.append(prob)
        place = jnp.concatenate(places, axis=1)
        prob = jnp.concatenate(probs, axis=1)
        for s in range(16):
            chosen = place[s : s + 1, :] == kk
            dmat[p, s] = jnp.where(chosen, 1.0, 0.0).astype(BF16)
            wmat[p, s] = jnp.where(chosen, prob[s : s + 1, :], 0.0).astype(BF16)
        return carry

    lax.fori_loop(0, PAIRS, routing, 0)

    pltpu.make_async_copy(rs_recv, rs_recv, rs_sems.at[1]).wait()
    total = resb[...].astype(F32) + own_part
    for d in range(7):
        total = total + rs_recv[d].astype(F32)
    mixed[...] = total
    gain = gain_ref[:, pl.ds(pl.multiple_of(blk * 256, 256), 256)]
    xg[0] = (total * gain).astype(BF16)
    sq_send[...] = lax.dot_general(
        jnp.ones((8, 256), F32),
        total * total,
        (((1,), (1,)), ((), ())),
        preferred_element_type=F32,
        precision=lax.Precision.HIGHEST,
    )

    def share_squares(d, carry):
        to = lax.rem(blk + d, 8)
        remote(
            sq_send,
            sq_recv.at[d - 1],
            sq_sems.at[0],
            sq_sems.at[1],
            (req, lax.div(to, 2), lax.rem(to, 2)),
        ).start()
        return carry

    lax.fori_loop(1, 8, share_squares, 0)
    for pos in range(1, NZ):
        remote(
            xg.at[0], xg.at[pos], xg_send.at[pos], xg_recv.at[pos], z_peer(NZ - ORDER[pos])
        ).start()
    pltpu.make_async_copy(sq_recv, sq_recv, sq_sems.at[1]).wait()
    squares = sq_send[...]
    for d in range(7):
        squares = squares + sq_recv[d]
    sc[0] = lax.rsqrt(squares * (1.0 / 2048.0) + 1e-6)
    for pos in range(1, NZ):
        remote(
            sc.at[0], sc.at[pos], sc_send.at[pos], sc_recv.at[pos], z_peer(NZ - ORDER[pos])
        ).start()

    for p in range(PAIRS):
        scaled = []
        for pos in (2 * p, 2 * p + 1):
            if pos:
                device = z_peer(NZ - ORDER[pos])
                remote(xg.at[0], xg.at[pos], xg_send.at[pos], xg_recv.at[pos], device).wait()
                remote(sc.at[0], sc.at[pos], sc_send.at[pos], sc_recv.at[pos], device).wait()
            factor = jnp.broadcast_to(sc[pos, 0:1, :], (128, 128)).T
            both = jnp.concatenate([factor, factor], axis=1)
            scaled.append((xg[pos].astype(F32) * both).astype(BF16))
        rows = jnp.concatenate(scaled, axis=0)
        picked = jnp.dot(dmat[p].reshape(768, 256), rows, preferred_element_type=F32)
        send1[p] = picked.astype(BF16).reshape(16, 2 * CAP, 256)

        def dispatch(d, carry, p=p):
            xh_to, xl_to, y_to, device = plane_peer(d)
            remote(
                send1.at[p, xh_to * 8 + xl_to * 4 + y_to],
                recv1.at[p, blk, xh],
                a2a_send.at[p],
                a2a_recv.at[p],
                device,
            ).start()
            return carry

        lax.fori_loop(1, 16, dispatch, 0)
        pltpu.make_async_copy(send1.at[p, slot], recv1.at[p, blk, xh], a2a_recv.at[p]).start()

    for i, (_, dst) in enumerate(weights):
        pltpu.make_async_copy(dst.at[c], dst.at[c], w_in.at[i]).wait()

    @pl.when(swap == 1)
    def _():
        for i, (_, dst) in enumerate(weights):
            remote(dst.at[c], dst.at[c], fwd_send.at[i], w_other.at[i], other_core).start()

    for i, (_, dst) in enumerate(weights):
        pltpu.make_async_copy(dst.at[1 - c], dst.at[1 - c], w_other.at[i]).wait()

    for p in range(PAIRS):
        pltpu.make_async_copy(recv1.at[p], recv1.at[p], a2a_recv.at[p]).wait()
        rows = jnp.concatenate(
            [recv1[p, b].reshape(4 * CAP, 256) for b in range(8)], axis=1
        )
        out = None
        for half in range(2):
            gate = jnp.dot(rows, wg[half], preferred_element_type=F32)
            up = jnp.dot(rows, wu[half], preferred_element_type=F32)
            act = (gate / (1.0 + jnp.exp(-gate)) * up).astype(BF16)
            down = jnp.dot(act, wd[half], preferred_element_type=F32)
            out = down if out is None else out + down
        for b in range(8):
            piece = out[:, b * 256 : (b + 1) * 256].astype(BF16)
            send2[p, b] = piece.reshape(2, 2 * CAP, 256)

        def give_back(d, carry, p=p):
            xh_to, xl_to, y_to, device = plane_peer(d)
            remote(
                send2.at[p, y_to * 2 + xl_to, xh_to],
                recv2.at[p, slot],
                back_send.at[p],
                back_recv.at[p],
                device,
            ).start()
            return carry

        lax.fori_loop(1, 16, give_back, 0)
        pltpu.make_async_copy(send2.at[p, blk, xh], recv2.at[p, slot], back_recv.at[p]).start()

    for p in range(PAIRS):
        pltpu.make_async_copy(recv2.at[p], recv2.at[p], back_recv.at[p]).wait()
        part = lax.dot_general(
            wmat[p].reshape(768, 256),
            recv2[p].reshape(768, 256),
            (((0,), (0,)), ((), ())),
            preferred_element_type=F32,
        )
        for r in range(2):
            pos = 2 * p + r
            piece = part[r * 128 : (r + 1) * 128, :]
            if pos == 0:
                own_sum[...] = piece
            else:
                zs_send[pos - 1] = piece.astype(BF16)
                remote(
                    zs_send.at[pos - 1],
                    zs_recv.at[pos - 1],
                    zs_sems.at[0],
                    zs_sems.at[1],
                    z_peer(ORDER[pos]),
                ).start()
    pltpu.make_async_copy(zs_recv, zs_recv, zs_sems.at[1]).wait()
    total = mixed[...] + own_sum[...]
    for d in range(7):
        total = total + zs_recv[d].astype(F32)
    out_ref[...] = total.astype(BF16)

    pltpu.make_async_copy(rs_send, rs_send, rs_sems.at[0]).wait()
    pltpu.make_async_copy(sq_recv, sq_recv, sq_sems.at[0]).wait()
    pltpu.make_async_copy(zs_send, zs_send, zs_sems.at[0]).wait()
    for p in range(PAIRS):
        sent = send1.at[p, pl.ds(0, 15)]
        pltpu.make_async_copy(sent, sent, a2a_send.at[p]).wait()
        sent = recv2.at[p, pl.ds(0, 15)]
        pltpu.make_async_copy(sent, sent, back_send.at[p]).wait()
    for i, (src, dst) in enumerate(weights):
        pltpu.make_async_copy(dst.at[c], dst.at[c], w_send.at[i]).wait()

    @pl.when(swap == 1)
    def _():
        for i, (_, dst) in enumerate(weights):
            pltpu.make_async_copy(dst.at[c], dst.at[c], fwd_send.at[i]).wait()


def shards(
    queries,
    keys,
    values,
    lengths,
    out_weight,
    residual,
    norm_gain,
    expert_ids,
    gate_weights,
    replica_map,
    w_gate,
    w_up,
    w_down,
):
    route = jnp.concatenate([expert_ids.T.astype(F32), gate_weights.T], axis=0)
    vmem = pl.BlockSpec(memory_space=pltpu.VMEM)
    hbm = pl.BlockSpec(memory_space=pl.ANY)
    dma = pltpu.SemaphoreType.DMA
    return pl.pallas_call(
        layer_kernel,
        out_shape=jax.ShapeDtypeStruct((128, 256), BF16),
        in_specs=[vmem] * 5 + [hbm] * 7,
        out_specs=vmem,
        scratch_shapes=[
            pltpu.VMEM((4096, 128), BF16),
            pltpu.VMEM((4096, 128), BF16),
            pltpu.VMEM((8, 256, 256), BF16),
            pltpu.VMEM((128, 256), BF16),
            pltpu.VMEM((128, 128), F32),
            pltpu.VMEM((128, 128), F32),
            pltpu.VMEM((2, 64, 256), BF16),
            pltpu.VMEM((2, 64, 256), BF16),
            pltpu.VMEM((7, 128, 256), BF16),
            pltpu.VMEM((7, 128, 256), BF16),
            pltpu.VMEM((128, 256), F32),
            pltpu.VMEM((8, 128), F32),
            pltpu.VMEM((7, 8, 128), F32),
            pltpu.VMEM((8, 8, 128), F32),
            pltpu.VMEM((8, 16, 128), F32),
            pltpu.VMEM((8, 128, 256), BF16),
            pltpu.VMEM((PAIRS, 16, 2 * CAP, 256), BF16),
            pltpu.VMEM((PAIRS, 16, 2 * CAP, 256), BF16),
            pltpu.VMEM((PAIRS, 16, 2 * CAP, 256), BF16),
            pltpu.VMEM((PAIRS, 8, 2, 2 * CAP, 256), BF16),
            pltpu.VMEM((PAIRS, 8, 2, 2 * CAP, 256), BF16),
            pltpu.VMEM((PAIRS, 16, 2 * CAP, 256), BF16),
            pltpu.VMEM((128, 256), F32),
            pltpu.VMEM((7, 128, 256), BF16),
            pltpu.VMEM((7, 128, 256), BF16),
            pltpu.VMEM((2, 2048, 192), BF16),
            pltpu.VMEM((2, 2048, 192), BF16),
            pltpu.VMEM((2, 192, 2048), BF16),
            dma((11,)),
            dma((3,)),
            dma((3,)),
            dma((3,)),
            dma((3,)),
            dma((2,)),
            dma((2,)),
            dma((2,)),
            dma((8,)),
            dma((8,)),
            dma((8,)),
            dma((8,)),
            dma((8,)),
            dma((8,)),
            dma((PAIRS,)),
            dma((PAIRS,)),
            dma((PAIRS,)),
            dma((PAIRS,)),
            dma((2,)),
        ],
        compiler_params=pltpu.CompilerParams(
            collective_id=0, has_side_effects=True, vmem_limit_bytes=56 * 2**20
        ),
        name="layer",
    )(
        queries,
        lengths.reshape(1, 128),
        norm_gain.reshape(1, 2048),
        route,
        replica_map.reshape(1, 128),
        keys.reshape(4096, 128),
        values.reshape(4096, 128),
        out_weight,
        residual,
        w_gate.reshape(2048, 192),
        w_up.reshape(2048, 192),
        w_down.reshape(192, 2048),
    )


def solution(mesh):
    in_specs = (
        P(("req", "exp"), "kvh"),
        P(("req", "exp"), "kvh", None, None),
        P(("req", "exp"), "kvh", None, None),
        P("req"),
        P(("kvh", "exp"), None),
        P("req", None),
        P(),
        P("req", None),
        P("req", None),
        P(),
        P(("req", "kvh"), None, "exp"),
        P(("req", "kvh"), None, "exp"),
        P(("req", "kvh"), "exp", None),
    )
    out_specs = P("req", ("kvh", "exp"))
    return jax.shard_map(shards, mesh=mesh, in_specs=in_specs, out_specs=out_specs, check_vma=False)
```

time: 419 us -> 117 us (0.28)
  waiting for transfers between devices: 244 us -> 0 us
  Pallas kernels: 0 us -> 109 us
  blocking collectives: 52.3 us -> 0 us
  local copies, waits for them, and re-layouts: 48.4 us -> 6.43 us
  other arithmetic: 25.5 us -> 0.6 us
  starting transfers between devices: 20.6 us -> 0 us
  matrix products: 14.3 us -> 0 us
  between operations: 13.5 us -> 0.01 us
    all_to_all x2 -> x0, waiting for transfers between devices: 110 us -> none  [the longest x1 71.3 us: shards(): lax.all_to_all(jnp.where(source[:, None] >= 0, taken, jnp.zeros((), jnp.b...]
    pallas_call x0 -> x1, Pallas kernels: none -> 109 us  [shards(): pl.pallas_call(layer_kernel, out_shape=jax.ShapeDtypeStruct((128, 256), B...]
    unnamed x4 -> x0, waiting for transfers between devices: 94 us -> none
    reduce_scatter x2 -> x0, waiting for transfers between devices: 39.6 us -> none  [the longest x1 20.8 us: shards(): lax.psum_scatter(partial_value.reshape(n_rows, n_kvh, block).astype(jnp.b...]
    all_gather x2 -> x0, blocking collectives: 33 us -> none  [the longest x1 28 us: shards(): full_rows = lax.all_gather(normed, ('kvh', 'exp'), axis=1, tiled=True)]
    all_to_all x2 -> x0, starting transfers between devices: 20.3 us -> none  [the longest x1 10.2 us: shards(): lax.all_to_all(jnp.where(source[:, None] >= 0, taken, jnp.zeros((), jnp.b...]
    psum x1 -> x0, blocking collectives: 19.3 us -> none  [shards(): squares = lax.psum(jnp.sum(mixed * mixed, axis=1), ('kvh', 'exp'))]
    another operation x5 -> x0, other arithmetic: 14.9 us -> none
  transfers between devices with their start and end apart: 5 -> 0, of which waited for: 5 -> 0; matrix products, arithmetic and copies ran while one was open for 6% -> 0% of each run, Pallas kernels for 0% -> 0%
where the time goes in v1:
time: 117 us
  Pallas kernels  109 us (93%)
  local copies, waits for them, and re-layouts  6.43 us (5%)
    pallas_call x1, Pallas kernels, shards(): pl.pallas_call(layer_kernel, out_shape=jax.ShapeDtypeStruct((128, 256), B...  109 us
    unnamed x9, local copies, waits for them, and re-layouts  6.43 us

profile of v1, /device:TPU:6, one launch (start us, length us, event | category | flops | bytes accessed | tf_op | source)
XLA Modules:
  0.0 116.5 jit_solution(205656339262123710)
XLA Ops:
  0.0 0.0 copy-start.1
  0.0 0.7 copy-done.1
  0.7 0.0 copy-start.2
  0.7 0.7 copy-done.2
  1.4 0.6 pad_maximum_fusion.route_ref
  2.0 0.0 copy-start
  2.0 2.3 %copy.14 = bf16[1,2048,192]{2,1,0:T(8,128)(2,1)} copy(bf16[1,2048,192]{1,2,0:T(8,128)(2,1)} %param.23) | data formatting | bytes 1572864 | tf_op args[10]
  4.3 0.0 copy-done
  4.3 1.3 %copy.15 = bf16[1,2048,192]{2,1,0:T(8,128)(2,1)} copy(bf16[1,2048,192]{1,2,0:T(8,128)(2,1)S(1)} %copy-done) | data formatting | bytes 1572864 | tf_op args[11]
  5.6 109.5 %layer.1 = bf16[128,256]{1,0:T(8,128)(2,1)} custom-call(bf16[64,512]{1,0:T(8,128)(2,1)} %q_ref.1, s32[1,128]{1,0:T(1,128)} %bitcast.18, f32[1,2048]{1,0:T(1,128)} %bitcast.16, f32[16,128]{1,0:T(8,128)} %pad_maximum_fusion.route_ref, s32[1,128]{1,0:T(1,128)} %bitcast.19, bf16[4096,128]{1,0:T(8,128)(2,1)} %bitcast.13, bf16[4096,128]{1,0:T(8,128)(2,1)} %bitcast.14, ...), custom_call_target="tpu_custom_call" | custom-call | tf_op jit(solution)/shard_map/layer/pallas_call | solution.py:430
  115.0 1.5 %copy.17 = bf16[128,256]{1,0:T(8,128)(2,1)} copy(bf16[128,256]{1,0:T(8,128)(2,1)} %layer.1) | data formatting | bytes 131072
  (1 shorter events, 0.0 us)
Async XLA Ops:
  0.0 0.7 copy-start.1
  0.7 0.7 copy-start.2
  2.0 2.3 %copy-start = (bf16[1,2048,192]{1,2,0:T(8,128)(2,1)S(1)}, bf16[1,2048,192]{1,2,0:T(8,128)(2,1)}, u32[]{:S(2)}) copy-start(bf16[1,2048,192]{1,2,0:T(8,128)(2,1)} %param.24) | copy-start | bytes 2359300

commit v2 on v1

v2 whole, which is shorter than its diff:
```python
import jax
import jax.numpy as jnp
from jax import lax
from jax.experimental import pallas as pl
from jax.experimental.pallas import tpu as pltpu
from jax.sharding import PartitionSpec as P

MESH = pl.DeviceIdType.MESH
F32 = jnp.float32
BF16 = jnp.bfloat16

NZ = 8
CAP = 24
ORDER = (0, 1, 7, 2, 6, 3, 5, 4)
PAIRS = NZ // 2


def layer_kernel(
    q_ref,
    len_ref,
    gain_ref,
    ids_ref,
    gates_ref,
    map_ref,
    k_hbm,
    v_hbm,
    ow_hbm,
    res_hbm,
    wg_hbm,
    wu_hbm,
    wd_hbm,
    out_ref,
    kbuf,
    vbuf,
    owb,
    resb,
    lens_t,
    eprim,
    att,
    oh,
    rs_send,
    rs_recv,
    mixed,
    sq_send,
    sq_recv,
    xraw,
    rt,
    xg,
    dmat,
    wmat,
    send1,
    recv1,
    send2,
    recv2,
    own_part,
    own_sum,
    xs_send,
    xs_recv,
    zs_send,
    zs_recv,
    wg,
    wu,
    wd,
    load_sem,
    w_send,
    w_in,
    fwd_send,
    w_other,
    att_sems,
    rs_sems,
    sq_sems,
    xraw_sems,
    rt_send,
    rt_recv,
    xg_send,
    xg_recv,
    a2a_send,
    a2a_recv,
    back_send,
    back_recv,
    xs_send_sem,
    xs_recv_sem,
    zs_sems,
):
    req = lax.axis_index("req")
    y = lax.axis_index("kvh")
    xl = lax.axis_index("exp")
    z = lax.div(req, 4)
    xh = lax.rem(lax.div(req, 2), 2)
    c = lax.rem(req, 2)
    blk = y * 2 + xl
    swap = lax.rem(c + xl, 2)

    def serve_peer(d):
        side = lax.div(d, 4)
        xh_to = lax.rem(xh + side, 2)
        xl_to = lax.rem(xl + side, 2)
        y_to = lax.rem(y + d, 4)
        return side, xh_to, y_to, (z * 4 + xh_to * 2 + c, y_to, xl_to)

    def group_peer(d):
        to = lax.rem(blk + d, 8)
        return to, (req, lax.div(to, 2), lax.rem(to, 2))

    def z_peer(d):
        return (lax.rem(z + d, NZ) * 4 + xh * 2 + c, y, xl)

    exp_peer = (req, y, 1 - xl)
    other_core = (z * 4 + xh * 2 + (1 - c), y, xl)
    swap_peer = (z * 4 + xh * 2 + (1 - c), y, 1 - xl)

    def remote(src, dst, send_sem, recv_sem, device):
        return pltpu.make_async_remote_copy(
            src_ref=src,
            dst_ref=dst,
            send_sem=send_sem,
            recv_sem=recv_sem,
            device_id=device,
            device_id_type=MESH,
        )

    barrier = pltpu.get_barrier_semaphore()

    def greet_group(d, carry):
        pl.semaphore_signal(barrier, inc=1, device_id=group_peer(d)[1], device_id_type=MESH)
        pl.semaphore_signal(barrier, inc=1, device_id=z_peer(d), device_id_type=MESH)
        return carry

    lax.fori_loop(1, 8, greet_group, 0)

    def greet_side(d, carry):
        pl.semaphore_signal(barrier, inc=1, device_id=serve_peer(d)[3], device_id_type=MESH)
        return carry

    lax.fori_loop(4, 8, greet_side, 0)
    pl.semaphore_signal(barrier, inc=1, device_id=other_core, device_id_type=MESH)

    @pl.when(swap == 1)
    def _():
        pl.semaphore_signal(barrier, inc=1, device_id=swap_peer, device_id_type=MESH)

    def load(src, dst, i):
        return pltpu.make_async_copy(src, dst, load_sem.at[i])

    loads = [load(k_hbm, kbuf, 0), load(v_hbm, vbuf, 1)]
    loads.append(
        load(res_hbm.at[:, pl.ds(pl.multiple_of(blk * 256, 256), 256)], resb, 2)
    )
    for b in range(8):
        loads.append(load(ow_hbm.at[:, pl.ds(b * 256, 256)], owb.at[b], 3 + b))
    for one in loads:
        one.start()
    rt[0, 0:8, :] = ids_ref[...].astype(F32)
    rt[0, 8:16, :] = gates_ref[...]
    lens_t[...] = jnp.broadcast_to(len_ref[...].astype(F32), (128, 128)).T

    row = jnp.broadcast_to(map_ref[...].astype(F32), (128, 128))
    col = row.T
    sub = lax.broadcasted_iota(jnp.int32, (128, 128), 0)
    lane = lax.broadcasted_iota(jnp.int32, (128, 128), 1)
    again = jnp.where((row == col) & (lane < sub), 1.0, 0.0)
    eprim[...] = jnp.where(jnp.max(again, axis=1, keepdims=True) > 0.0, -1.0, col)

    loads[0].wait()
    loads[1].wait()
    scale = 128 ** (-0.5)
    rows_at = lax.broadcasted_iota(jnp.int32, (64, 1024), 0)
    cols_at = lax.broadcasted_iota(jnp.int32, (64, 1024), 1)
    same = (rows_at & 15) == (cols_at >> 6)
    at = (cols_at & 63).astype(F32)
    for g in range(4):
        lo = g * 16
        heads = [q_ref[lo : lo + 16, h * 128 : (h + 1) * 128] for h in range(4)]
        q16 = jnp.concatenate(heads, axis=0)
        k16 = kbuf[g * 1024 : (g + 1) * 1024, :]
        s = lax.dot_general(q16, k16, (((1,), (1,)), ((), ())), preferred_element_type=F32)
        own_len = lens_t[pl.ds(pl.multiple_of(xl * 64 + lo, 16), 16), :][:, 0:1]
        live = same & (at < jnp.concatenate([own_len] * 4, axis=0))
        s = jnp.where(live, s * scale, -1e30)
        peak = jnp.max(s, axis=1, keepdims=True)
        w = jnp.where(live, jnp.exp(s - peak), 0.0)
        total = jnp.sum(w, axis=1, keepdims=True)
        v16 = vbuf[g * 1024 : (g + 1) * 1024, :]
        a = jnp.dot(w.astype(BF16), v16, preferred_element_type=F32) / total
        a = a.astype(BF16)
        for h in range(4):
            att[h // 2, lo : lo + 16, (h % 2) * 128 : (h % 2 + 1) * 128] = a[
                h * 16 : (h + 1) * 16, :
            ]
    oh[xl] = att[xl]

    pl.semaphore_wait(barrier, 19 + swap)
    att_copy = remote(att.at[1 - xl], oh.at[xl], att_sems.at[0], att_sems.at[1], exp_peer)
    att_copy.start()

    weights = ((wg_hbm, wg), (wu_hbm, wu), (wd_hbm, wd))

    def swap_pieces(first, last):
        @pl.when(swap == 1)
        def _():
            for piece in range(first, last):
                i, part = piece // 4, pl.ds(piece % 4 * 48, 48)
                src, dst = weights[i]
                remote(
                    src.at[part], dst.at[1 - c, part], w_send.at[i], w_in.at[i], swap_peer
                ).start()

    swap_pieces(0, 1)

    @pl.when(swap == 0)
    def _():
        for i, (src, dst) in enumerate(weights):
            pltpu.make_async_copy(src, dst.at[c], w_in.at[i]).start()
            remote(src, dst.at[c], w_send.at[i], w_other.at[i], other_core).start()

    for pos in range(1, NZ):
        remote(
            rt.at[0], rt.at[pos], rt_send.at[pos], rt_recv.at[pos], z_peer(NZ - ORDER[pos])
        ).start()

    for i in range(2, 11):
        loads[i].wait()
    att_copy.wait()
    heads_all = oh[...].reshape(128, 256)

    def scatter(d, carry):
        to, device = group_peer(d)
        part = jnp.dot(heads_all, owb[to], preferred_element_type=F32)
        rs_send[d - 1] = part.astype(BF16)
        remote(
            rs_send.at[d - 1], rs_recv.at[d - 1], rs_sems.at[0], rs_sems.at[1], device
        ).start()
        return carry

    lax.fori_loop(1, 8, scatter, 0)
    swap_pieces(1, 3)
    own_out = jnp.dot(heads_all, owb[blk], preferred_element_type=F32)

    for pos in range(1, NZ):
        remote(
            rt.at[0], rt.at[pos], rt_send.at[pos], rt_recv.at[pos], z_peer(NZ - ORDER[pos])
        ).wait()
    first_slot = z * 16 + xh * 8 + xl * 4
    side_slot = z * 16 + (1 - xh) * 8 + (1 - xl) * 4
    expert = jnp.concatenate(
        [eprim[pl.ds(first_slot + i, 1), :] for i in range(4)]
        + [eprim[pl.ds(side_slot + i, 1), :] for i in range(4)],
        axis=0,
    )
    upper = jnp.where(sub < lane, 1.0, 0.0).astype(BF16)
    kk = lax.broadcasted_iota(jnp.int32, (2 * CAP, 256), 0).astype(F32)

    def routing(p, carry):
        places, probs = [], []
        for r in range(2):
            info = rt[2 * p + r]
            ids = info[0:8, :]
            gates = info[8:16, :]
            top = gates / jnp.sum(gates, axis=0, keepdims=True)
            named = jnp.zeros((8, 128), F32)
            prob = jnp.zeros((8, 128), F32)
            for j in range(8):
                hit = ids[j : j + 1, :] == expert
                named = jnp.where(hit, 1.0, named)
                prob = jnp.where(hit, top[j : j + 1, :], prob)
            before = jnp.dot(named.astype(BF16), upper, preferred_element_type=F32)
            places.append(jnp.where(named > 0.0, before + r * CAP, -100.0))
            probs.append(prob)
        place = jnp.concatenate(places, axis=1)
        prob = jnp.concatenate(probs, axis=1)
        for s in range(8):
            chosen = place[s : s + 1, :] == kk
            dmat[p, s] = jnp.where(chosen, 1.0, 0.0).astype(BF16)
            wmat[p, s] = jnp.where(chosen, prob[s : s + 1, :], 0.0).astype(BF16)
        return carry

    lax.fori_loop(0, PAIRS, routing, 0)

    pltpu.make_async_copy(rs_recv, rs_recv, rs_sems.at[1]).wait()
    total = resb[...].astype(F32) + own_out
    for d in range(7):
        total = total + rs_recv[d].astype(F32)
    mixed[...] = total
    sq_send[...] = lax.dot_general(
        jnp.ones((8, 256), F32),
        total * total,
        (((1,), (1,)), ((), ())),
        preferred_element_type=F32,
        precision=lax.Precision.HIGHEST,
    )

    def share_squares(d, carry):
        remote(
            sq_send, sq_recv.at[d - 1], sq_sems.at[0], sq_sems.at[1], group_peer(d)[1]
        ).start()
        return carry

    lax.fori_loop(1, 8, share_squares, 0)
    gain = gain_ref[:, pl.ds(pl.multiple_of(blk * 256, 256), 256)]
    xraw[xl] = (total * gain).astype(BF16)
    xraw_copy = remote(xraw.at[xl], xraw.at[xl], xraw_sems.at[0], xraw_sems.at[1], exp_peer)
    xraw_copy.start()
    swap_pieces(3, 12)
    pltpu.make_async_copy(sq_recv, sq_recv, sq_sems.at[1]).wait()
    squares = sq_send[...]
    for d in range(7):
        squares = squares + sq_recv[d]
    factor = lax.rsqrt(squares * (1.0 / 2048.0) + 1e-6)
    factor = jnp.broadcast_to(factor[0:1, :], (128, 128)).T
    factor = jnp.concatenate([factor, factor], axis=1)
    xraw_copy.wait()
    for half in range(2):
        xg[0, half] = (xraw[half].astype(F32) * factor).astype(BF16)

    def onward(pos_from, pos_to, step):
        return remote(
            xg.at[pos_from], xg.at[pos_to], xg_send.at[pos_to], xg_recv.at[pos_to], z_peer(step)
        )

    place_of = {offset: pos for pos, offset in enumerate(ORDER)}
    hops = {}
    for k in range(4):
        hops[place_of[k + 1]] = onward(place_of[k], place_of[k + 1], NZ - 1)
    for k in range(3):
        hops[place_of[NZ - 1 - k]] = onward(
            place_of[(NZ - k) % NZ], place_of[NZ - 1 - k], 1
        )
    hops[1].start()
    hops[2].start()

    for p in range(PAIRS):
        for pos in (2 * p + 1, 2 * p + 2):
            if pos < NZ:
                hops[pos].wait_recv()
                if pos + 2 < NZ:
                    hops[pos + 2].start()
        for half in range(2):
            rows = xg[2 * p : 2 * p + 2, half].reshape(256, 256)
            picked = jnp.dot(dmat[p].reshape(384, 256), rows, preferred_element_type=F32)
            send1[p, :, :, half * 256 : (half + 1) * 256] = picked.astype(BF16).reshape(
                8, 2 * CAP, 256
            )

        def dispatch(d, carry, p=p):
            side, _, y_to, device = serve_peer(d)
            remote(
                send1.at[p, side * 4 + y_to],
                recv1.at[p, y, xh],
                a2a_send.at[p],
                a2a_recv.at[p],
                device,
            ).start()
            return carry

        lax.fori_loop(1, 8, dispatch, 0)
        pltpu.make_async_copy(send1.at[p, y], recv1.at[p, y, xh], a2a_recv.at[p]).start()

    for i, (_, dst) in enumerate(weights):
        pltpu.make_async_copy(dst.at[c], dst.at[c], w_in.at[i]).wait()

        @pl.when(swap == 1)
        def _(i=i, dst=dst):
            remote(dst.at[c], dst.at[c], fwd_send.at[i], w_other.at[i], other_core).start()

    for i, (_, dst) in enumerate(weights):
        pltpu.make_async_copy(dst.at[1 - c], dst.at[1 - c], w_other.at[i]).wait()

    contract = (((1,), (1,)), ((), ()))
    for p in reversed(range(PAIRS)):
        pltpu.make_async_copy(recv1.at[p], recv1.at[p], a2a_recv.at[p]).wait()
        rows = jnp.concatenate(
            [recv1[p, b].reshape(4 * CAP, 512) for b in range(4)], axis=1
        )
        out = None
        for half in range(2):
            gate = lax.dot_general(rows, wg[half], contract, preferred_element_type=F32)
            up = lax.dot_general(rows, wu[half], contract, preferred_element_type=F32)
            act = (gate / (1.0 + jnp.exp(-gate)) * up).astype(BF16)
            down = jnp.dot(act, wd[half], preferred_element_type=F32)
            out = down if out is None else out + down
        for b in range(4):
            piece = out[:, b * 512 : (b + 1) * 512].astype(BF16)
            send2[p, b] = piece.reshape(2, 2 * CAP, 512)

        def give_back(d, carry, p=p):
            side, xh_to, y_to, device = serve_peer(d)
            remote(
                send2.at[p, y_to, xh_to],
                recv2.at[p, side * 4 + y],
                back_send.at[p],
                back_recv.at[p],
                device,
            ).start()
            return carry

        lax.fori_loop(1, 8, give_back, 0)
        pltpu.make_async_copy(send2.at[p, y, xh], recv2.at[p, y], back_recv.at[p]).start()

    def xs_copy(p):
        return remote(
            xs_send.at[p], xs_recv.at[p], xs_send_sem.at[p], xs_recv_sem.at[p], exp_peer
        )

    def to_owner(p):
        xs_copy(p).wait_recv()
        for r in range(2):
            pos = 2 * p + r
            piece = own_part[p, r] + xs_recv[p, r].astype(F32)
            if pos == 0:
                own_sum[...] = piece
            else:
                zs_send[pos - 1] = piece.astype(BF16)
                remote(
                    zs_send.at[pos - 1],
                    zs_recv.at[pos - 1],
                    zs_sems.at[0],
                    zs_sems.at[1],
                    z_peer(ORDER[pos]),
                ).start()

    for p in reversed(range(PAIRS)):
        pltpu.make_async_copy(recv2.at[p], recv2.at[p], back_recv.at[p]).wait()
        part = lax.dot_general(
            wmat[p].reshape(384, 256),
            recv2[p].reshape(384, 512),
            (((0,), (0,)), ((), ())),
            preferred_element_type=F32,
        )
        first, second = part[:, 0:256], part[:, 256:512]
        own_part[p] = jnp.where(xl == 0, first, second).reshape(2, 128, 256)
        xs_send[p] = jnp.where(xl == 0, second, first).astype(BF16).reshape(2, 128, 256)
        xs_copy(p).start()
        if p < PAIRS - 1:
            to_owner(p + 1)
    to_owner(0)

    pltpu.make_async_copy(zs_recv, zs_recv, zs_sems.at[1]).wait()
    total = mixed[...] + own_sum[...]
    for d in range(7):
        total = total + zs_recv[d].astype(F32)
    out_ref[...] = total.astype(BF16)

    pltpu.make_async_copy(rs_send, rs_send, rs_sems.at[0]).wait()
    pltpu.make_async_copy(sq_recv, sq_recv, sq_sems.at[0]).wait()
    pltpu.make_async_copy(zs_send, zs_send, zs_sems.at[0]).wait()
    for pos in range(1, NZ):
        hops[pos].wait_send()
    for p in range(PAIRS):
        xs_copy(p).wait_send()
        sent = send1.at[p, pl.ds(0, 7)]
        pltpu.make_async_copy(sent, sent, a2a_send.at[p]).wait()
        sent = recv2.at[p, pl.ds(0, 7)]
        pltpu.make_async_copy(sent, sent, back_send.at[p]).wait()
    for i, (src, dst) in enumerate(weights):
        pltpu.make_async_copy(dst.at[c], dst.at[c], w_send.at[i]).wait()

    @pl.when(swap == 1)
    def _():
        for i, (_, dst) in enumerate(weights):
            pltpu.make_async_copy(dst.at[c], dst.at[c], fwd_send.at[i]).wait()


def shards(
    queries,
    keys,
    values,
    lengths,
    out_weight,
    residual,
    norm_gain,
    expert_ids,
    gate_weights,
    replica_map,
    w_gate,
    w_up,
    w_down,
):
    vmem = pl.BlockSpec(memory_space=pltpu.VMEM)
    hbm = pl.BlockSpec(memory_space=pl.ANY)
    dma = pltpu.SemaphoreType.DMA
    return pl.pallas_call(
        layer_kernel,
        out_shape=jax.ShapeDtypeStruct((128, 256), BF16),
        in_specs=[vmem] * 6 + [hbm] * 7,
        out_specs=vmem,
        scratch_shapes=[
            pltpu.VMEM((4096, 128), BF16),
            pltpu.VMEM((4096, 128), BF16),
            pltpu.VMEM((8, 256, 256), BF16),
            pltpu.VMEM((128, 256), BF16),
            pltpu.VMEM((128, 128), F32),
            pltpu.VMEM((128, 128), F32),
            pltpu.VMEM((2, 64, 256), BF16),
            pltpu.VMEM((2, 64, 256), BF16),
            pltpu.VMEM((7, 128, 256), BF16),
            pltpu.VMEM((7, 128, 256), BF16),
            pltpu.VMEM((128, 256), F32),
            pltpu.VMEM((8, 128), F32),
            pltpu.VMEM((7, 8, 128), F32),
            pltpu.VMEM((2, 128, 256), BF16),
            pltpu.VMEM((8, 16, 128), F32),
            pltpu.VMEM((8, 2, 128, 256), BF16),
            pltpu.VMEM((PAIRS, 8, 2 * CAP, 256), BF16),
            pltpu.VMEM((PAIRS, 8, 2 * CAP, 256), BF16),
            pltpu.VMEM((PAIRS, 8, 2 * CAP, 512), BF16),
            pltpu.VMEM((PAIRS, 4, 2, 2 * CAP, 512), BF16),
            pltpu.VMEM((PAIRS, 4, 2, 2 * CAP, 512), BF16),
            pltpu.VMEM((PAIRS, 8, 2 * CAP, 512), BF16),
            pltpu.VMEM((PAIRS, 2, 128, 256), F32),
            pltpu.VMEM((128, 256), F32),
            pltpu.VMEM((PAIRS, 2, 128, 256), BF16),
            pltpu.VMEM((PAIRS, 2, 128, 256), BF16),
            pltpu.VMEM((7, 128, 256), BF16),
            pltpu.VMEM((7, 128, 256), BF16),
            pltpu.VMEM((2, 192, 2048), BF16),
            pltpu.VMEM((2, 192, 2048), BF16),
            pltpu.VMEM((2, 192, 2048), BF16),
            dma((11,)),
            dma((3,)),
            dma((3,)),
            dma((3,)),
            dma((3,)),
            dma((2,)),
            dma((2,)),
            dma((2,)),
            dma((2,)),
            dma((8,)),
            dma((8,)),
            dma((8,)),
            dma((8,)),
            dma((PAIRS,)),
            dma((PAIRS,)),
            dma((PAIRS,)),
            dma((PAIRS,)),
            dma((PAIRS,)),
            dma((PAIRS,)),
            dma((2,)),
        ],
        compiler_params=pltpu.CompilerParams(
            collective_id=0, has_side_effects=True, vmem_limit_bytes=56 * 2**20
        ),
        name="layer",
    )(
        queries,
        lengths.reshape(1, 128),
        norm_gain.reshape(1, 2048),
        expert_ids.T,
        gate_weights.T,
        replica_map.reshape(1, 128),
        keys.reshape(4096, 128),
        values.reshape(4096, 128),
        out_weight,
        residual,
        w_gate.reshape(2048, 192).T,
        w_up.reshape(2048, 192).T,
        w_down.reshape(192, 2048),
    )


def solution(mesh):
    in_specs = (
        P(("req", "exp"), "kvh"),
        P(("req", "exp"), "kvh", None, None),
        P(("req", "exp"), "kvh", None, None),
        P("req"),
        P(("kvh", "exp"), None),
        P("req", None),
        P(),
        P("req", None),
        P("req", None),
        P(),
        P(("req", "kvh"), None, "exp"),
        P(("req", "kvh"), None, "exp"),
        P(("req", "kvh"), "exp", None),
    )
    out_specs = P("req", ("kvh", "exp"))
    return jax.shard_map(shards, mesh=mesh, in_specs=in_specs, out_specs=out_specs, check_vma=False)
```

time: 117 us -> 82.8 us (0.71)
  Pallas kernels: 109 us -> 80.2 us
  local copies, waits for them, and re-layouts: 6.43 us -> 1.47 us
    pallas_call x1, Pallas kernels: 109 us -> 80.2 us  [shards(): pl.pallas_call(layer_kernel, out_shape=jax.ShapeDtypeStruct((128, 256), B...]
    unnamed x9 -> x1, local copies, waits for them, and re-layouts: 6.43 us -> 1.47 us
where the time goes in v2:
time: 82.8 us; the launch traced here: 81.7 us
  Pallas kernels  80.2 us (97%)
  local copies, waits for them, and re-layouts  1.47 us (2%)
    pallas_call x1, Pallas kernels, shards(): pl.pallas_call(layer_kernel, out_shape=jax.ShapeDtypeStruct((128, 256), B...  80.2 us

profile of v2, /device:TPU:6, one launch (start us, length us, event | category | flops | bytes accessed | tf_op | source)
XLA Modules:
  0.0 81.7 jit_solution(15749928204687725558)
XLA Ops:
  0.0 80.2 %layer.1 = bf16[128,256]{1,0:T(8,128)(2,1)} custom-call(bf16[64,512]{1,0:T(8,128)(2,1)} %q_ref.1, s32[1,128]{1,0:T(1,128)} %bitcast.22, f32[1,2048]{1,0:T(1,128)} %bitcast.19, s32[8,128]{1,0:T(8,128)} %bitcast.20, f32[8,128]{1,0:T(8,128)} %bitcast.21, s32[1,128]{1,0:T(1,128)} %bitcast.23, bf16[4096,128]{1,0:T(8,128)(2,1)} %bitcast.14, ...), custom_call_target="tpu_custom_call" | custom-call | tf_op jit(solution)/shard_map/layer/pallas_call | solution.py:481
  80.2 1.5 %copy.15 = bf16[128,256]{1,0:T(8,128)(2,1)} copy(bf16[128,256]{1,0:T(8,128)(2,1)} %layer.1) | data formatting | bytes 131072

commit v3 on v2

--- a/solution.py
+++ b/solution.py
@@ -13,6 +13,7 @@
 CAP = 24
 ORDER = (0, 1, 7, 2, 6, 3, 5, 4)
 PAIRS = NZ // 2
+BLOCKS = (1, 3, 2, 0)
 
 
 def layer_kernel(
@@ -43,7 +44,7 @@
     mixed,
     sq_send,
     sq_recv,
-    xraw,
+    sc,
     rt,
     xg,
     dmat,
@@ -53,23 +54,28 @@
     send2,
     recv2,
     own_part,
-    own_sum,
     xs_send,
     xs_recv,
     zs_send,
     zs_recv,
+    zx_recv,
     wg,
     wu,
     wd,
+    act,
     load_sem,
     w_send,
     w_in,
     fwd_send,
     w_other,
     att_sems,
-    rs_sems,
+    rs_send_sem,
+    rs_recv_sem,
     sq_sems,
-    xraw_sems,
+    pair_send,
+    pair_recv,
+    sc_send,
+    sc_recv,
     rt_send,
     rt_recv,
     xg_send,
@@ -80,7 +86,9 @@
     back_recv,
     xs_send_sem,
     xs_recv_sem,
-    zs_sems,
+    zs_send_sem,
+    zs_recv_sem,
+    zx_sems,
 ):
     req = lax.axis_index("req")
     y = lax.axis_index("kvh")
@@ -92,7 +100,7 @@
     swap = lax.rem(c + xl, 2)
 
     def serve_peer(d):
-        side = lax.div(d, 4)
+        side = d // 4 if isinstance(d, int) else lax.div(d, 4)
         xh_to = lax.rem(xh + side, 2)
         xl_to = lax.rem(xl + side, 2)
         y_to = lax.rem(y + d, 4)
@@ -106,6 +114,8 @@
         return (lax.rem(z + d, NZ) * 4 + xh * 2 + c, y, xl)
 
     exp_peer = (req, y, 1 - xl)
+    cross_up = (lax.rem(z + 1, NZ) * 4 + xh * 2 + c, y, 1 - xl)
+    cross_down = (lax.rem(z + NZ - 1, NZ) * 4 + xh * 2 + c, y, 1 - xl)
     other_core = (z * 4 + xh * 2 + (1 - c), y, xl)
     swap_peer = (z * 4 + xh * 2 + (1 - c), y, 1 - xl)
 
@@ -133,7 +143,8 @@
         return carry
 
     lax.fori_loop(4, 8, greet_side, 0)
-    pl.semaphore_signal(barrier, inc=1, device_id=other_core, device_id_type=MESH)
+    for device in (other_core, cross_up, cross_down):
+        pl.semaphore_signal(barrier, inc=1, device_id=device, device_id_type=MESH)
 
     @pl.when(swap == 1)
     def _():
@@ -189,29 +200,38 @@
             ]
     oh[xl] = att[xl]
 
-    pl.semaphore_wait(barrier, 19 + swap)
+    pl.semaphore_wait(barrier, 21 + swap)
     att_copy = remote(att.at[1 - xl], oh.at[xl], att_sems.at[0], att_sems.at[1], exp_peer)
     att_copy.start()
 
-    weights = ((wg_hbm, wg), (wu_hbm, wu), (wd_hbm, wd))
+    weights = ((wg_hbm, wg), (wu_hbm, wu))
+
+    def down_columns(k):
+        return pl.ds(pl.multiple_of(lax.rem(y + k, 4) * 512, 512), 512)
 
     def swap_pieces(first, last):
         @pl.when(swap == 1)
         def _():
             for piece in range(first, last):
-                i, part = piece // 4, pl.ds(piece % 4 * 48, 48)
-                src, dst = weights[i]
-                remote(
-                    src.at[part], dst.at[1 - c, part], w_send.at[i], w_in.at[i], swap_peer
-                ).start()
-
-    swap_pieces(0, 1)
+                if piece < 12:
+                    i, part = piece // 6, pl.ds(piece % 6 * 32, 32)
+                    src, dst = weights[i]
+                    src, dst = src.at[part], dst.at[1 - c, part]
+                else:
+                    k = BLOCKS[piece - 12]
+                    i, src, dst = 2 + k, wd_hbm.at[:, down_columns(k)], wd.at[1 - c, k]
+                remote(src, dst, w_send.at[i], w_in.at[i], swap_peer).start()
+
 
     @pl.when(swap == 0)
     def _():
         for i, (src, dst) in enumerate(weights):
             pltpu.make_async_copy(src, dst.at[c], w_in.at[i]).start()
             remote(src, dst.at[c], w_send.at[i], w_other.at[i], other_core).start()
+        for k in BLOCKS:
+            src, dst = wd_hbm.at[:, down_columns(k)], wd.at[c, k]
+            pltpu.make_async_copy(src, dst, w_in.at[2 + k]).start()
+            remote(src, dst, w_send.at[2 + k], w_other.at[2 + k], other_core).start()
 
     for pos in range(1, NZ):
         remote(
@@ -223,17 +243,29 @@
     att_copy.wait()
     heads_all = oh[...].reshape(128, 256)
 
+    def scatter_copy(j, d):
+        return remote(
+            rs_send.at[j, d - 1],
+            rs_recv.at[j, d - 1],
+            rs_send_sem.at[j],
+            rs_recv_sem.at[j],
+            group_peer(d)[1],
+        )
+
     def scatter(d, carry):
-        to, device = group_peer(d)
-        part = jnp.dot(heads_all, owb[to], preferred_element_type=F32)
-        rs_send[d - 1] = part.astype(BF16)
-        remote(
-            rs_send.at[d - 1], rs_recv.at[d - 1], rs_sems.at[0], rs_sems.at[1], device
-        ).start()
+        part = jnp.dot(heads_all, owb[group_peer(d)[0]], preferred_element_type=F32)
+        part = part.astype(BF16)
+        rs_send[0, d - 1] = part[0:64, :]
+        scatter_copy(0, d).start()
+        rs_send[1, d - 1] = part[64:128, :]
         return carry
 
+    def scatter_rest(d, carry):
+        scatter_copy(1, d).start()
+        return carry
+
     lax.fori_loop(1, 8, scatter, 0)
-    swap_pieces(1, 3)
+    lax.fori_loop(1, 8, scatter_rest, 0)
     own_out = jnp.dot(heads_all, owb[blk], preferred_element_type=F32)
 
     for pos in range(1, NZ):
@@ -276,18 +308,24 @@
 
     lax.fori_loop(0, PAIRS, routing, 0)
 
-    pltpu.make_async_copy(rs_recv, rs_recv, rs_sems.at[1]).wait()
-    total = resb[...].astype(F32) + own_out
-    for d in range(7):
-        total = total + rs_recv[d].astype(F32)
-    mixed[...] = total
-    sq_send[...] = lax.dot_general(
-        jnp.ones((8, 256), F32),
-        total * total,
-        (((1,), (1,)), ((), ())),
-        preferred_element_type=F32,
-        precision=lax.Precision.HIGHEST,
-    )
+    def onward(pos_from, pos_to, step, j):
+        return remote(
+            xg.at[pos_from, j],
+            xg.at[pos_to, j],
+            xg_send.at[pos_to, j],
+            xg_recv.at[pos_to, j],
+            z_peer(step),
+        )
+
+    place_of = {offset: pos for pos, offset in enumerate(ORDER)}
+    hops = {}
+    for j in range(2):
+        for k in range(4 - j):
+            hops[place_of[k + 1], j] = onward(place_of[k], place_of[k + 1], NZ - 1, j)
+        for k in range(3 + j):
+            hops[place_of[NZ - 1 - k], j] = onward(
+                place_of[(NZ - k) % NZ], place_of[NZ - 1 - k], 1, j
+            )
 
     def share_squares(d, carry):
         remote(
@@ -295,47 +333,74 @@
         ).start()
         return carry
 
-    lax.fori_loop(1, 8, share_squares, 0)
+    def pair_copy(j):
+        part = xg.at[0, j, xl]
+        return remote(part, part, pair_send.at[j], pair_recv.at[j], exp_peer)
+
     gain = gain_ref[:, pl.ds(pl.multiple_of(blk * 256, 256), 256)]
-    xraw[xl] = (total * gain).astype(BF16)
-    xraw_copy = remote(xraw.at[xl], xraw.at[xl], xraw_sems.at[0], xraw_sems.at[1], exp_peer)
-    xraw_copy.start()
-    swap_pieces(3, 12)
+    for j in range(2):
+        pltpu.make_async_copy(rs_recv.at[j], rs_recv.at[j], rs_recv_sem.at[j]).wait()
+        tokens = slice(64 * j, 64 * j + 64)
+        total = resb[tokens, :].astype(F32) + own_out[tokens, :]
+        for d in range(7):
+            total = total + rs_recv[j, d].astype(F32)
+        mixed[tokens, :] = total
+        xg[0, j, xl] = (total * gain).astype(BF16)
+        pair_copy(j).start()
+        if j:
+            total = mixed[...]
+            sq_send[...] = lax.dot_general(
+                jnp.ones((8, 256), F32),
+                total * total,
+                (((1,), (1,)), ((), ())),
+                preferred_element_type=F32,
+                precision=lax.Precision.HIGHEST,
+            )
+            lax.fori_loop(1, 8, share_squares, 0)
+            swap_pieces(0, 16)
+    for j in range(2):
+        pair_copy(j).wait_recv()
+        hops[1, j].start()
+        hops[2, j].start()
     pltpu.make_async_copy(sq_recv, sq_recv, sq_sems.at[1]).wait()
     squares = sq_send[...]
     for d in range(7):
         squares = squares + sq_recv[d]
-    factor = lax.rsqrt(squares * (1.0 / 2048.0) + 1e-6)
-    factor = jnp.broadcast_to(factor[0:1, :], (128, 128)).T
-    factor = jnp.concatenate([factor, factor], axis=1)
-    xraw_copy.wait()
-    for half in range(2):
-        xg[0, half] = (xraw[half].astype(F32) * factor).astype(BF16)
-
-    def onward(pos_from, pos_to, step):
+    sc[0] = lax.rsqrt(squares * (1.0 / 2048.0) + 1e-6)
+
+    def scale_copy(pos):
         return remote(
-            xg.at[pos_from], xg.at[pos_to], xg_send.at[pos_to], xg_recv.at[pos_to], z_peer(step)
-        )
-
-    place_of = {offset: pos for pos, offset in enumerate(ORDER)}
-    hops = {}
-    for k in range(4):
-        hops[place_of[k + 1]] = onward(place_of[k], place_of[k + 1], NZ - 1)
-    for k in range(3):
-        hops[place_of[NZ - 1 - k]] = onward(
-            place_of[(NZ - k) % NZ], place_of[NZ - 1 - k], 1
-        )
-    hops[1].start()
-    hops[2].start()
-
+            sc.at[0], sc.at[pos], sc_send.at[pos], sc_recv.at[pos], z_peer(NZ - ORDER[pos])
+        )
+
+    for pos in range(1, NZ):
+        scale_copy(pos).start()
+
+    forwards = {
+        (1, 0): 3, (2, 0): 4, (1, 1): 3, (2, 1): 4, (3, 0): 5, (4, 0): 6,
+        (3, 1): 5, (4, 1): 6, (5, 0): 7, (6, 1): 7,
+    }
     for p in range(PAIRS):
-        for pos in (2 * p + 1, 2 * p + 2):
-            if pos < NZ:
-                hops[pos].wait_recv()
-                if pos + 2 < NZ:
-                    hops[pos + 2].start()
+        arrive = [pos for pos in (2 * p + 1, 2 * p + 2) if pos < NZ]
+        for j in range(2):
+            for pos in arrive:
+                hops[pos, j].wait_recv()
+                if (pos, j) in forwards:
+                    hops[forwards[pos, j], j].start()
+        scaled = []
+        for pos in (2 * p, 2 * p + 1):
+            if pos:
+                scale_copy(pos).wait_recv()
+            factor = jnp.broadcast_to(sc[pos, 0:1, :], (128, 128)).T
+            factor = jnp.concatenate([factor, factor], axis=1)
+            scaled.append(
+                [
+                    (xg[pos, :, h].reshape(128, 256).astype(F32) * factor).astype(BF16)
+                    for h in range(2)
+                ]
+            )
         for half in range(2):
-            rows = xg[2 * p : 2 * p + 2, half].reshape(256, 256)
+            rows = jnp.concatenate([scaled[0][half], scaled[1][half]], axis=0)
             picked = jnp.dot(dmat[p].reshape(384, 256), rows, preferred_element_type=F32)
             send1[p, :, :, half * 256 : (half + 1) * 256] = picked.astype(BF16).reshape(
                 8, 2 * CAP, 256
@@ -355,70 +420,58 @@
         lax.fori_loop(1, 8, dispatch, 0)
         pltpu.make_async_copy(send1.at[p, y], recv1.at[p, y, xh], a2a_recv.at[p]).start()
 
-    for i, (_, dst) in enumerate(weights):
-        pltpu.make_async_copy(dst.at[c], dst.at[c], w_in.at[i]).wait()
+    def share(i, mine, other):
+        pltpu.make_async_copy(mine, mine, w_in.at[i]).wait()
 
         @pl.when(swap == 1)
-        def _(i=i, dst=dst):
-            remote(dst.at[c], dst.at[c], fwd_send.at[i], w_other.at[i], other_core).start()
-
-    for i, (_, dst) in enumerate(weights):
-        pltpu.make_async_copy(dst.at[1 - c], dst.at[1 - c], w_other.at[i]).wait()
-
+        def _():
+            remote(mine, mine, fwd_send.at[i], w_other.at[i], other_core).start()
+
+        return pltpu.make_async_copy(other, other, w_other.at[i])
+
+    for one in [share(i, dst.at[c], dst.at[1 - c]) for i, (_, dst) in enumerate(weights)]:
+        one.wait()
     contract = (((1,), (1,)), ((), ()))
-    for p in reversed(range(PAIRS)):
+
+    def hidden(p):
         pltpu.make_async_copy(recv1.at[p], recv1.at[p], a2a_recv.at[p]).wait()
         rows = jnp.concatenate(
             [recv1[p, b].reshape(4 * CAP, 512) for b in range(4)], axis=1
         )
-        out = None
         for half in range(2):
             gate = lax.dot_general(rows, wg[half], contract, preferred_element_type=F32)
             up = lax.dot_general(rows, wu[half], contract, preferred_element_type=F32)
-            act = (gate / (1.0 + jnp.exp(-gate)) * up).astype(BF16)
-            down = jnp.dot(act, wd[half], preferred_element_type=F32)
-            out = down if out is None else out + down
-        for b in range(4):
-            piece = out[:, b * 512 : (b + 1) * 512].astype(BF16)
-            send2[p, b] = piece.reshape(2, 2 * CAP, 512)
-
-        def give_back(d, carry, p=p):
-            side, xh_to, y_to, device = serve_peer(d)
-            remote(
-                send2.at[p, y_to, xh_to],
-                recv2.at[p, side * 4 + y],
-                back_send.at[p],
-                back_recv.at[p],
-                device,
-            ).start()
-            return carry
-
-        lax.fori_loop(1, 8, give_back, 0)
-        pltpu.make_async_copy(send2.at[p, y, xh], recv2.at[p, y], back_recv.at[p]).start()
+            act[p, half] = (gate / (1.0 + jnp.exp(-gate)) * up).astype(BF16)
+
+    def down_block(p, k):
+        out = jnp.dot(act[p, 0], wd[0, k], preferred_element_type=F32)
+        out = out + jnp.dot(act[p, 1], wd[1, k], preferred_element_type=F32)
+        send2[p, k] = out.astype(BF16).reshape(2, 2 * CAP, 512)
+        for d in (k, 4 + k):
+            side, xh_to, _, device = serve_peer(d)
+            src, dst = send2.at[p, k, xh_to], recv2.at[p, side * 4 + y]
+            if d == 0:
+                pltpu.make_async_copy(src, dst, back_recv.at[p]).start()
+            else:
+                remote(src, dst, back_send.at[p], back_recv.at[p], device).start()
+
+    hidden(0)
+    hidden(1)
+    hidden(2)
+    for k in BLOCKS:
+        share(2 + k, wd.at[c, k], wd.at[1 - c, k]).wait()
+        down_block(2, k)
+    hidden(3)
+    for p in (3, 1, 0):
+        for k in BLOCKS:
+            down_block(p, k)
 
     def xs_copy(p):
         return remote(
             xs_send.at[p], xs_recv.at[p], xs_send_sem.at[p], xs_recv_sem.at[p], exp_peer
         )
 
-    def to_owner(p):
-        xs_copy(p).wait_recv()
-        for r in range(2):
-            pos = 2 * p + r
-            piece = own_part[p, r] + xs_recv[p, r].astype(F32)
-            if pos == 0:
-                own_sum[...] = piece
-            else:
-                zs_send[pos - 1] = piece.astype(BF16)
-                remote(
-                    zs_send.at[pos - 1],
-                    zs_recv.at[pos - 1],
-                    zs_sems.at[0],
-                    zs_sems.at[1],
-                    z_peer(ORDER[pos]),
-                ).start()
-
-    for p in reversed(range(PAIRS)):
+    def combine(p):
         pltpu.make_async_copy(recv2.at[p], recv2.at[p], back_recv.at[p]).wait()
         part = lax.dot_general(
             wmat[p].reshape(384, 256),
@@ -429,35 +482,88 @@
         first, second = part[:, 0:256], part[:, 256:512]
         own_part[p] = jnp.where(xl == 0, first, second).reshape(2, 128, 256)
         xs_send[p] = jnp.where(xl == 0, second, first).astype(BF16).reshape(2, 128, 256)
-        xs_copy(p).start()
-        if p < PAIRS - 1:
-            to_owner(p + 1)
-    to_owner(0)
-
-    pltpu.make_async_copy(zs_recv, zs_recv, zs_sems.at[1]).wait()
-    total = mixed[...] + own_sum[...]
-    for d in range(7):
-        total = total + zs_recv[d].astype(F32)
+
+    sent_up = {1: 1, 2: NZ - 1, 3: 2, 4: NZ - 1, 5: 1, 6: NZ - 2, 7: 2}
+    added = {2: (4, 6), 3: (5, 7)}
+
+    def z_copy(pos):
+        i = pos - 1
+        return remote(
+            zs_send.at[i],
+            zs_recv.at[i],
+            zs_send_sem.at[i],
+            zs_recv_sem.at[i],
+            z_peer(sent_up[pos]),
+        )
+
+    def pass_on(pos, cross):
+        piece = own_part[pos // 2, pos % 2]
+        if cross:
+            piece = piece + xs_recv[pos // 2, pos % 2].astype(F32)
+        for other in added.get(pos, ()):
+            z_copy(other).wait_recv()
+            piece = piece + zs_recv[other - 1].astype(F32)
+        zs_send[pos - 1] = piece.astype(BF16)
+        z_copy(pos).start()
+
+    last_copy = remote(
+        xs_send.at[0, 0], xs_recv.at[0, 0], xs_send_sem.at[0], xs_recv_sem.at[0], exp_peer
+    )
+    cross_copy = remote(xs_send.at[0, 1], zx_recv, zx_sems.at[0], zx_sems.at[1], cross_up)
+    combine(2)
+    xs_copy(2).start()
+    combine(3)
+    xs_copy(3).start()
+    for p in (2, 3):
+        xs_copy(p).wait_recv()
+        pass_on(2 * p, True)
+        pass_on(2 * p + 1, True)
+    combine(1)
+    xs_copy(1).start()
+    combine(0)
+    cross_copy.start()
+    last_copy.start()
+    pass_on(1, False)
+    xs_copy(1).wait_recv()
+    pass_on(3, True)
+    pass_on(2, True)
+    total = mixed[...] + own_part[0, 0]
+    last_copy.wait_recv()
+    total = total + xs_recv[0, 0].astype(F32)
+    cross_copy.wait_recv()
+    total = total + zx_recv[...].astype(F32)
+    for pos in (1, 2, 3):
+        z_copy(pos).wait_recv()
+        total = total + zs_recv[pos - 1].astype(F32)
     out_ref[...] = total.astype(BF16)
 
-    pltpu.make_async_copy(rs_send, rs_send, rs_sems.at[0]).wait()
+    for j in range(2):
+        pltpu.make_async_copy(rs_send.at[j], rs_send.at[j], rs_send_sem.at[j]).wait()
+        pair_copy(j).wait_send()
     pltpu.make_async_copy(sq_recv, sq_recv, sq_sems.at[0]).wait()
-    pltpu.make_async_copy(zs_send, zs_send, zs_sems.at[0]).wait()
     for pos in range(1, NZ):
-        hops[pos].wait_send()
+        z_copy(pos).wait_send()
+    last_copy.wait_send()
+    cross_copy.wait_send()
+    for pos in range(1, NZ):
+        hops[pos, 0].wait_send()
+        hops[pos, 1].wait_send()
+        scale_copy(pos).wait_send()
     for p in range(PAIRS):
-        xs_copy(p).wait_send()
+        if p:
+            xs_copy(p).wait_send()
         sent = send1.at[p, pl.ds(0, 7)]
         pltpu.make_async_copy(sent, sent, a2a_send.at[p]).wait()
         sent = recv2.at[p, pl.ds(0, 7)]
         pltpu.make_async_copy(sent, sent, back_send.at[p]).wait()
-    for i, (src, dst) in enumerate(weights):
-        pltpu.make_async_copy(dst.at[c], dst.at[c], w_send.at[i]).wait()
+    halves = [wg.at[c], wu.at[c]] + [wd.at[c, k] for k in range(4)]
+    for i, half in enumerate(halves):
+        pltpu.make_async_copy(half, half, w_send.at[i]).wait()
 
     @pl.when(swap == 1)
     def _():
-        for i, (_, dst) in enumerate(weights):
-            pltpu.make_async_copy(dst.at[c], dst.at[c], fwd_send.at[i]).wait()
+        for i, half in enumerate(halves):
+            pltpu.make_async_copy(half, half, fwd_send.at[i]).wait()
 
 
 def shards(
@@ -492,14 +598,14 @@
             pltpu.VMEM((128, 128), F32),
             pltpu.VMEM((2, 64, 256), BF16),
             pltpu.VMEM((2, 64, 256), BF16),
-            pltpu.VMEM((7, 128, 256), BF16),
-            pltpu.VMEM((7, 128, 256), BF16),
+            pltpu.VMEM((2, 7, 64, 256), BF16),
+            pltpu.VMEM((2, 7, 64, 256), BF16),
             pltpu.VMEM((128, 256), F32),
             pltpu.VMEM((8, 128), F32),
             pltpu.VMEM((7, 8, 128), F32),
-            pltpu.VMEM((2, 128, 256), BF16),
+            pltpu.VMEM((8, 8, 128), F32),
             pltpu.VMEM((8, 16, 128), F32),
-            pltpu.VMEM((8, 2, 128, 256), BF16),
+            pltpu.VMEM((8, 2, 2, 64, 256), BF16),
             pltpu.VMEM((PAIRS, 8, 2 * CAP, 256), BF16),
             pltpu.VMEM((PAIRS, 8, 2 * CAP, 256), BF16),
             pltpu.VMEM((PAIRS, 8, 2 * CAP, 512), BF16),
@@ -507,19 +613,22 @@
             pltpu.VMEM((PAIRS, 4, 2, 2 * CAP, 512), BF16),
             pltpu.VMEM((PAIRS, 8, 2 * CAP, 512), BF16),
             pltpu.VMEM((PAIRS, 2, 128, 256), F32),
-            pltpu.VMEM((128, 256), F32),
             pltpu.VMEM((PAIRS, 2, 128, 256), BF16),
             pltpu.VMEM((PAIRS, 2, 128, 256), BF16),
             pltpu.VMEM((7, 128, 256), BF16),
             pltpu.VMEM((7, 128, 256), BF16),
+            pltpu.VMEM((128, 256), BF16),
             pltpu.VMEM((2, 192, 2048), BF16),
             pltpu.VMEM((2, 192, 2048), BF16),
-            pltpu.VMEM((2, 192, 2048), BF16),
+            pltpu.VMEM((2, 4, 192, 512), BF16),
+            pltpu.VMEM((PAIRS, 2, 4 * CAP, 192), BF16),
             dma((11,)),
-            dma((3,)),
-            dma((3,)),
-            dma((3,)),
-            dma((3,)),
+            dma((6,)),
+            dma((6,)),
+            dma((6,)),
+            dma((6,)),
+            dma((2,)),
+            dma((2,)),
             dma((2,)),
             dma((2,)),
             dma((2,)),
@@ -528,12 +637,16 @@
             dma((8,)),
             dma((8,)),
             dma((8,)),
+            dma((8, 2)),
+            dma((8, 2)),
             dma((PAIRS,)),
             dma((PAIRS,)),
             dma((PAIRS,)),
             dma((PAIRS,)),
             dma((PAIRS,)),
             dma((PAIRS,)),
+            dma((7,)),
+            dma((7,)),
             dma((2,)),
         ],
         compiler_params=pltpu.CompilerParams(

time: 82.8 us -> 78.8 us (0.952)
  Pallas kernels: 80.2 us -> 77 us
    pallas_call x1, Pallas kernels: 80.2 us -> 77 us  [shards(): pl.pallas_call(layer_kernel, out_shape=jax.ShapeDtypeStruct((128, 256), B...]
where the time goes in v3:
time: 78.8 us; the launch traced here: 78.5 us
  Pallas kernels  77 us (98%)
  local copies, waits for them, and re-layouts  1.47 us (2%)
    pallas_call x1, Pallas kernels, shards(): pl.pallas_call(layer_kernel, out_shape=jax.ShapeDtypeStruct((128, 256), B...  77 us

profile of v3, /device:TPU:6, one launch (start us, length us, event | category | flops | bytes accessed | tf_op | source)
XLA Modules:
  0.0 78.5 jit_solution(6554631563403122137)
XLA Ops:
  0.0 77.0 %layer.1 = bf16[128,256]{1,0:T(8,128)(2,1)} custom-call(bf16[64,512]{1,0:T(8,128)(2,1)} %q_ref.1, s32[1,128]{1,0:T(1,128)} %bitcast.22, f32[1,2048]{1,0:T(1,128)} %bitcast.19, s32[8,128]{1,0:T(8,128)} %bitcast.20, f32[8,128]{1,0:T(8,128)} %bitcast.21, s32[1,128]{1,0:T(1,128)} %bitcast.23, bf16[4096,128]{1,0:T(8,128)(2,1)} %bitcast.14, ...), custom_call_target="tpu_custom_call" | custom-call | tf_op jit(solution)/shard_map/layer/pallas_call | solution.py:587
  77.0 1.5 %copy.15 = bf16[128,256]{1,0:T(8,128)(2,1)} copy(bf16[128,256]{1,0:T(8,128)(2,1)} %layer.1) | data formatting | bytes 131072

commit v4 on v3

--- a/solution.py
+++ b/solution.py
@@ -213,12 +213,11 @@
         @pl.when(swap == 1)
         def _():
             for piece in range(first, last):
-                if piece < 12:
-                    i, part = piece // 6, pl.ds(piece % 6 * 32, 32)
-                    src, dst = weights[i]
-                    src, dst = src.at[part], dst.at[1 - c, part]
+                if piece < 2:
+                    i = piece
+                    src, dst = weights[i][0], weights[i][1].at[1 - c]
                 else:
-                    k = BLOCKS[piece - 12]
+                    k = BLOCKS[piece - 2]
                     i, src, dst = 2 + k, wd_hbm.at[:, down_columns(k)], wd.at[1 - c, k]
                 remote(src, dst, w_send.at[i], w_in.at[i], swap_peer).start()
 
@@ -357,7 +356,7 @@
                 precision=lax.Precision.HIGHEST,
             )
             lax.fori_loop(1, 8, share_squares, 0)
-            swap_pieces(0, 16)
+            swap_pieces(0, 6)
     for j in range(2):
         pair_copy(j).wait_recv()
         hops[1, j].start()
@@ -521,9 +520,9 @@
     combine(1)
     xs_copy(1).start()
     combine(0)
-    cross_copy.start()
     last_copy.start()
     pass_on(1, False)
+    cross_copy.start()
     xs_copy(1).wait_recv()
     pass_on(3, True)
     pass_on(2, True)

time: 78.8 us -> 78.6 us (level)
  no operation moved by 1% of the time
where the time goes in v4:
time: 78.6 us; the launch traced here: 78.5 us
  Pallas kernels  77 us (98%)
  local copies, waits for them, and re-layouts  1.47 us (2%)
    pallas_call x1, Pallas kernels, shards(): pl.pallas_call(layer_kernel, out_shape=jax.ShapeDtypeStruct((128, 256), B...  77 us

profile of v4, /device:TPU:6, one launch (start us, length us, event | category | flops | bytes accessed | tf_op | source)
XLA Modules:
  0.0 78.5 jit_solution(16730639224557439510)
XLA Ops:
  0.0 77.0 %layer.1 = bf16[128,256]{1,0:T(8,128)(2,1)} custom-call(bf16[64,512]{1,0:T(8,128)(2,1)} %q_ref.1, s32[1,128]{1,0:T(1,128)} %bitcast.22, f32[1,2048]{1,0:T(1,128)} %bitcast.19, s32[8,128]{1,0:T(8,128)} %bitcast.20, f32[8,128]{1,0:T(8,128)} %bitcast.21, s32[1,128]{1,0:T(1,128)} %bitcast.23, bf16[4096,128]{1,0:T(8,128)(2,1)} %bitcast.14, ...), custom_call_target="tpu_custom_call" | custom-call | tf_op jit(solution)/shard_map/layer/pallas_call | solution.py:586
  77.0 1.5 %copy.15 = bf16[128,256]{1,0:T(8,128)(2,1)} copy(bf16[128,256]{1,0:T(8,128)(2,1)} %layer.1) | data formatting | bytes 131072

commit v5 on v4

--- a/solution.py
+++ b/solution.py
@@ -222,15 +222,16 @@
                 remote(src, dst, w_send.at[i], w_in.at[i], swap_peer).start()
 
 
-    @pl.when(swap == 0)
-    def _():
-        for i, (src, dst) in enumerate(weights):
-            pltpu.make_async_copy(src, dst.at[c], w_in.at[i]).start()
-            remote(src, dst.at[c], w_send.at[i], w_other.at[i], other_core).start()
-        for k in BLOCKS:
-            src, dst = wd_hbm.at[:, down_columns(k)], wd.at[c, k]
-            pltpu.make_async_copy(src, dst, w_in.at[2 + k]).start()
-            remote(src, dst, w_send.at[2 + k], w_other.at[2 + k], other_core).start()
+    def keep_weights():
+        @pl.when(swap == 0)
+        def _():
+            for i, (src, dst) in enumerate(weights):
+                pltpu.make_async_copy(src, dst.at[c], w_in.at[i]).start()
+                remote(src, dst.at[c], w_send.at[i], w_other.at[i], other_core).start()
+            for k in BLOCKS:
+                src, dst = wd_hbm.at[:, down_columns(k)], wd.at[c, k]
+                pltpu.make_async_copy(src, dst, w_in.at[2 + k]).start()
+                remote(src, dst, w_send.at[2 + k], w_other.at[2 + k], other_core).start()
 
     for pos in range(1, NZ):
         remote(
@@ -357,6 +358,7 @@
             )
             lax.fori_loop(1, 8, share_squares, 0)
             swap_pieces(0, 6)
+            keep_weights()
     for j in range(2):
         pair_copy(j).wait_recv()
         hops[1, j].start()

time: 78.6 us -> 78.6 us (level)
  no operation moved by 1% of the time
where the time goes in v5:
time: 78.6 us; the launch traced here: 78.5 us
  Pallas kernels  77 us (98%)
  local copies, waits for them, and re-layouts  1.47 us (2%)
    pallas_call x1, Pallas kernels, shards(): pl.pallas_call(layer_kernel, out_shape=jax.ShapeDtypeStruct((128, 256), B...  77 us

profile of v5, /device:TPU:6, one launch (start us, length us, event | category | flops | bytes accessed | tf_op | source)
XLA Modules:
  0.0 78.5 jit_solution(16310720981196096105)
XLA Ops:
  0.0 77.0 %layer.1 = bf16[128,256]{1,0:T(8,128)(2,1)} custom-call(bf16[64,512]{1,0:T(8,128)(2,1)} %q_ref.1, s32[1,128]{1,0:T(1,128)} %bitcast.22, f32[1,2048]{1,0:T(1,128)} %bitcast.19, s32[8,128]{1,0:T(8,128)} %bitcast.20, f32[8,128]{1,0:T(8,128)} %bitcast.21, s32[1,128]{1,0:T(1,128)} %bitcast.23, bf16[4096,128]{1,0:T(8,128)(2,1)} %bitcast.14, ...), custom_call_target="tpu_custom_call" | custom-call | tf_op jit(solution)/shard_map/layer/pallas_call | solution.py:588
  77.0 1.5 %copy.15 = bf16[128,256]{1,0:T(8,128)(2,1)} copy(bf16[128,256]{1,0:T(8,128)(2,1)} %layer.1) | data formatting | bytes 131072
